TPU v7x, 1024 devices: a whole 8x8x8 slice. The times are simulated.
1024 devices in a mesh: seq: 64 (over y, x), head: 16 (over z, core).
Axes of the slice: x: 8, y: 8, z: 8, core: 2. Of those that a mesh axis runs over, the one named last changes fastest.
Arguments:
- queries: bfloat16 [8192, 4096], P('seq', 'head'), may hold values from -64 to 64
- keys: bfloat16 [8192, 4096], P('seq', 'head'), may hold values from -8 to 8
- values: bfloat16 [8192, 4096], P('seq', 'head'), may hold values from -8 to 8
- gate: float32 [32], P('head'), may hold values from -6 to 6
- out_weight: bfloat16 [4096, 4096], P('head'), may hold values from -0.09375 to 0.09375
- out_grad: bfloat16 [8192, 4096], P('seq', 'head'), may hold values from -6 to 6
- valid: int32 [64], P('seq'), may hold values from 32 to 128, as said below
- starts: int32 [64], P('seq'), may hold values from 0 to 1, as said below
Outputs:
- output: bfloat16 [8192, 4096], P('seq', 'head')
- query_grad: bfloat16 [8192, 4096], P('seq', 'head')
- key_grad: bfloat16 [8192, 4096], P('seq', 'head')
- value_grad: bfloat16 [8192, 4096], P('seq', 'head')
Inputs may be any that keep to these rules, and one draw needn't show every extreme that they name: `valid`: A segment with fewer than 128 live tokens is followed by a segment that starts a document, or is the last one. The first segment starts a document and the second does not.
All inputs are finite; a program needn't handle non-finite values.
Results may differ from a plain program's by a relative error of at most 0.029.
Values may be sent and summed in bfloat16 or wider, within the bound.
A program may use at most 64 MiB of HBM per device.

v0:
```python
import jax
import jax.numpy as jnp
from jax import lax
from jax.sharding import PartitionSpec as P

DH = 128


precise = lax.Precision.HIGHEST


def carried_in(value, axis, join, neutral):
    count, mine = (lax.axis_size(axis), lax.axis_index(axis))
    pieces = jax.tree.map(lambda part: lax.all_gather(part, axis), value)
    total = jax.tree.map(
        lambda part, zero: jnp.full_like(part, 0) + jnp.asarray(zero, part.dtype), value, neutral
    )

    def carried_turn(position, total):
        longer = join(total, jax.tree.map(lambda part: part[position], pieces))
        return jax.tree.map(lambda new, old: jnp.where(position < mine, new, old), longer, total)

    return lax.fori_loop(0, count - 1, carried_turn, total)


def entering(shard, axis, combine, identity):
    devices, position = (lax.axis_size(axis), lax.axis_index(axis))
    everything = jax.tree.map(
        lambda part, kind: lax.all_gather(part.astype(kind), axis),
        shard,
        jax.tree.map(lambda a: jnp.bfloat16 if a.dtype == jnp.float32 else a.dtype, shard),
    )
    start = jax.tree.map(
        lambda part, zero: jnp.broadcast_to(jnp.asarray(zero, part.dtype), part.shape),
        shard,
        identity,
    )

    def entering_turn(k, before):
        at = devices - 1 - k
        reached = at > position
        new = combine(
            before, jax.tree.map(lambda part, own: part[at].astype(own.dtype), everything, shard)
        )
        return jax.tree.map(lambda a, b: jnp.where(reached, a, b), new, before)

    return lax.fori_loop(0, devices, entering_turn, start)


def feature_map(inputs):
    return jnp.where(inputs > 0, inputs + 1.0, jnp.exp(jnp.minimum(inputs, 0.0)))


def segment_state(key_vals, value_vals, live_mask):
    length = key_vals.shape[0]
    sig_keys = feature_map(key_vals.reshape(length, -1, DH)) * live_mask[:, None, None]
    val_heads = value_vals.reshape(length, -1, DH) * live_mask[:, None, None]
    memory = jnp.einsum("thd,the->hde", sig_keys, val_heads, precision=precise)
    return (memory, jnp.sum(sig_keys, axis=0))


def segment_read(query_vals, key_vals, value_vals, live_mask, memory, norm_sum, gate_weight):
    length = query_vals.shape[0]
    query_heads = query_vals.reshape(length, -1, DH)
    query_low = query_heads.astype(jnp.bfloat16)
    key_low = key_vals.reshape(length, -1, DH).astype(jnp.bfloat16)
    value_low = value_vals.reshape(length, -1, DH).astype(jnp.bfloat16)
    sig_query = feature_map(query_heads)
    numer = jnp.einsum("thd,hde->the", sig_query, memory, precision=precise)
    denom = jnp.einsum("thd,hd->th", sig_query, norm_sum, precision=precise) + 1.0
    memory_read = numer / denom[:, :, None]
    scores = jnp.einsum(
        "thd,shd->hts", query_low, key_low, preferred_element_type=jnp.float32
    ) * DH ** (-0.5)
    where_pos = jnp.arange(length)
    allowed = (where_pos[None, :] <= where_pos[:, None]) & (live_mask[None, :] > 0)
    scores = jnp.where(allowed[None], scores, -1e30)
    row_top = lax.stop_gradient(jnp.max(scores, axis=-1, keepdims=True))
    expo = jnp.exp(scores - row_top)
    probs = expo / jnp.sum(expo, axis=-1, keepdims=True)
    probs_low = probs.astype(jnp.bfloat16)
    local_read = jnp.einsum(
        "hts,she->the", probs_low, value_low, preferred_element_type=jnp.float32
    )
    mixed = (
        gate_weight[None, :, None] * memory_read + (1.0 - gate_weight)[None, :, None] * local_read
    )
    return (mixed * live_mask[:, None, None]).reshape(length, -1)


def join_forward(earlier, later):
    keep = 1.0 - later[0]
    return (
        jnp.maximum(earlier[0], later[0]),
        later[1] + keep * earlier[1],
        later[2] + keep * earlier[2],
    )


def join_reverse(earlier, later):
    keep = 1.0 - later[0]
    return (
        jnp.maximum(earlier[0], later[0]),
        later[1] + keep * earlier[1],
        later[2] + keep * earlier[2],
    )


def shards(queries, keys, values, gate, out_weight, out_grad, valid, starts):
    length = queries.shape[0]
    live_mask = (jnp.arange(length) < valid[0]).astype(jnp.float32)
    query_full = queries.astype(jnp.float32)
    key_full = keys.astype(jnp.float32)
    value_full = values.astype(jnp.float32)
    gate_weight = jax.nn.sigmoid(gate)
    start_flag = starts.astype(jnp.float32)
    opened = 1.0 - start_flag
    memory_local, norm_local = segment_state(key_full, value_full, live_mask)
    empty = (jnp.zeros((1,), jnp.float32), jnp.zeros_like(memory_local), jnp.zeros_like(norm_local))
    _, memory_prev, norm_prev = carried_in(
        (start_flag, memory_local, norm_local), "seq", join_forward, empty
    )
    memory_in = opened * memory_prev
    norm_in = opened * norm_prev

    def read_local(query_arg, key_arg, value_arg, memory_arg, norm_arg):
        return segment_read(
            query_arg, key_arg, value_arg, live_mask, memory_arg, norm_arg, gate_weight
        )

    mixed, pullback = jax.vjp(read_local, query_full, key_full, value_full, memory_in, norm_in)
    mixed_heads = mixed.astype(jnp.bfloat16)
    weight_part = out_weight
    projected = lax.psum_scatter(
        lax.dot_general(
            weight_part, mixed_heads, (((0,), (1,)), ((), ())), preferred_element_type=jnp.float32
        ),
        "head",
        scatter_dimension=0,
        tiled=True,
    ).T
    output = projected.astype(jnp.bfloat16)
    weight_part = out_weight
    mixed_grad = lax.dot_general(
        lax.all_gather(out_grad, "head", axis=1, tiled=True),
        weight_part,
        (((1,), (1,)), ((), ())),
        preferred_element_type=jnp.float32,
    )
    mixed_grad = lax.optimization_barrier(mixed_grad.astype(jnp.bfloat16)).astype(jnp.float32)
    query_part, key_part, value_part, memory_grad, norm_grad = pullback(mixed_grad)
    passed = (start_flag, opened * memory_grad, opened * norm_grad)
    _, memory_back, norm_back = entering(passed, "seq", join_reverse, empty)

    def state_local(key_arg, value_arg):
        return segment_state(key_arg, value_arg, live_mask)

    _, state_pull = jax.vjp(state_local, key_full, value_full)
    key_more, value_more = state_pull((memory_back, norm_back))
    query_grad = query_part.astype(jnp.bfloat16)
    key_grad = (key_part + key_more).astype(jnp.bfloat16)
    value_grad = (value_part + value_more).astype(jnp.bfloat16)
    return (output, query_grad, key_grad, value_grad)


def solution(mesh):
    placed = (
        P("seq", "head"),
        P("seq", "head"),
        P("seq", "head"),
        P("head"),
        P("head", None),
        P("seq", "head"),
        P("seq"),
        P("seq"),
    )
    return jax.shard_map(
        shards,
        mesh=mesh,
        in_specs=placed,
        out_specs=(P("seq", "head"), P("seq", "head"), P("seq", "head"), P("seq", "head")),
        check_vma=False,
    )
```

profile of v0, /device:TPU:14, one launch (start us, length us, event | category | flops | bytes accessed | tf_op | source)
XLA Modules:
  0.0 1033.9 jit_solution(30139464350786040)
XLA Ops:
  17.8 142.0 %all-reduce = f32[64]{0:T(128)} all-reduce(f32[64]{0:T(128)S(1)} %convert_dynamic-update-slice_fusion), channel_id=3, replica_groups=mesh['seq'=64,'head'=16] {'seq'}, use_global_device_ids=true, to_apply=%add | all-reduce | flops 64 | bytes 512
  159.8 56.1 %all_gather.44 = f32[64,2,128]{2,1,0:T(2,128)S(1)} all-gather(f32[1,2,128]{2,1,0:T(2,128)S(1)} %bitcast.178), channel_id=1, replica_groups=mesh['seq'=64,'head'=16] {'seq'}, dimensions={0}, use_global_device_ids=true | all-gather | bytes 66560 | tf_op jit(solution)/shard_map/all_gather | solution.py:14
  217.5 2.1 convolution_convert_fusion
  219.7 296.4 %while.34 = (s32[]{:T(128)}, f32[2,128,128]{2,1,0:T(8,128)S(1)}, f32[2,128]{1,0:T(2,128)}, s32[]{:T(128)}, f32[64,2,128,128]{3,2,1,0:T(8,128)}, /*index=5*/f32[6...) while((s32[]{:T(128)}, f32[2,128,128]{2,1,0:T(8,128)S(1)}, f32[2,128]{1,0:T(2,128)}, ...), condition=%wide.region_2.3_spmd.clone, body=%wide.region_1.2_spmd.clone.sunk | while | flops 132101 | bytes 396431 | solution.py:23
  520.8 2.6 convolution_bitcast_fusion
  529.5 130.7 %all-reduce.1 = bf16[64]{0:T(256)(128)(2,1)} all-reduce(bf16[64]{0:T(256)(128)(2,1)S(1)} %dynamic-update-slice.1), channel_id=5, replica_groups=mesh['seq'=64,'head'=16] {'seq'}, use_global_device_ids=true, to_apply=%add.1 | all-reduce | flops 64 | bytes 256
  669.1 51.4 %all-gather.5 = bf16[64,2,128]{2,1,0:T(2,128)(2,1)S(1)} all-gather(bf16[1,2,128]{2,1,0:T(2,128)(2,1)S(1)} %fusion.51), channel_id=6, replica_groups=mesh['seq'=64,'head'=16] {'seq'}, dimensions={0}, use_global_device_ids=true | all-gather | bytes 33280 | tf_op jit(solution)/shard_map/all_gather | solution.py:29
  722.0 302.2 %while.35 = (s32[]{:T(128)}, f32[2,128,128]{2,1,0:T(8,128)S(1)}, f32[2,128]{1,0:T(2,128)}, s32[]{:T(128)}, bf16[64,2,128,128]{3,2,1,0:T(8,128)(2,1)}, /*index=5*...) while((s32[]{:T(128)}, f32[2,128,128]{2,1,0:T(8,128)S(1)}, ...), condition=%wide.region_9.10_spmd.clone, body=%wide.region_8.9_spmd.clone.sunk | while | flops 165129 | bytes 330443 | solution.py:47
  728.9 1.9 fusion.92
  733.6 1.9 fusion.92
  738.3 1.9 fusion.92
  743.1 1.9 fusion.92
  747.8 1.9 fusion.92
  771.5 1.9 fusion.92
  776.2 1.9 fusion.92
  780.9 1.9 fusion.92
  785.7 1.9 fusion.92
  790.4 1.9 fusion.92
  818.8 1.9 fusion.92
  823.5 1.9 fusion.92
  828.3 1.9 fusion.92
  833.0 1.9 fusion.92
  837.7 1.9 fusion.92
  861.4 1.9 fusion.92
  866.1 1.9 fusion.92
  870.9 1.9 fusion.92
  875.6 1.9 fusion.92
  880.3 1.9 fusion.92
  908.7 1.9 fusion.92
  913.5 1.9 fusion.92
  918.2 1.9 fusion.92
  922.9 1.9 fusion.92
  (455 shorter events, 586.4 us)
Async XLA Ops:
  7.2 210.4 %copy-start = (bf16[256,4096]{1,0:T(8,128)(2,1)S(1)}, bf16[256,4096]{1,0:T(8,128)(2,1)}, u32[]{:S(2)}) copy-start(bf16[256,4096]{1,0:T(8,128)(2,1)} %param.16) | copy-start | bytes 6291460
  7.2 8.0 copy-start.1
  7.2 208.7 %copy-start.14 = (f32[2]{0:T(128)S(1)}, f32[2]{0:T(128)}, u32[]{:S(2)}) copy-start(f32[2]{0:T(128)} %param.15) | copy-start | bytes 28
  7.2 210.3 %all-gather.10.cloned.1.call-start = ((), (), s32[]{:S(2)}) async-start(), calls=%async_computation.2 | async-start | bytes 1114112 | tf_op jit(solution)/shard_map/all_gather | solution.py:145
  7.9 211.8 %all-gather.12.cloned.1.call-start = ((), (), s32[]{:S(2)}) async-start(), calls=%async_computation.3 | async-start | bytes 8519680 | tf_op jit(solution)/shard_map/all_gather | solution.py:14
  8.6 4.8 copy-start.6
  13.4 707.0 %reduce-scatter.2.cloned.1.call-start = ((), (), s32[]{:S(2)}) async-start(), calls=%async_computation.1 | async-start | bytes 2228224 | tf_op jit(solution)/shard_map/reduce_scatter | solution.py:134
  14.5 202.1 %copy-start.4 = (bf16[128,256]{0,1:T(8,128)(2,1)}, bf16[128,256]{0,1:T(8,128)(2,1)S(1)}, u32[]{:S(2)}) copy-start(bf16[128,256]{0,1:T(8,128)(2,1)S(1)} %copy.84) | copy-start | bytes 196612
  15.3 201.3 %copy-start.2 = (bf16[128,256]{0,1:T(8,128)(2,1)}, bf16[128,256]{0,1:T(8,128)(2,1)S(1)}, u32[]{:S(2)}) copy-start(bf16[128,256]{0,1:T(8,128)(2,1)S(1)} %copy.83) | copy-start | bytes 196612
  516.9 0.8 copy-start.10
  523.4 0.6 copy-start.7
  523.4 0.7 copy-start.12
  523.4 0.7 copy-start.13
  523.4 198.6 %all-gather.14.cloned.1.call-start = ((), (), s32[]{:S(2)}) async-start(), calls=%async_computation.4 | async-start | bytes 4259840 | tf_op jit(solution)/shard_map/all_gather | solution.py:29
  666.1 360.2 %copy-start.3 = (bf16[128,256]{0,1:T(8,128)(2,1)S(1)}, bf16[128,256]{0,1:T(8,128)(2,1)}, u32[]{:S(2)}) copy-start(bf16[128,256]{0,1:T(8,128)(2,1)} %copy-done.2) | copy-start | bytes 196612
  666.2 360.2 %copy-start.5 = (f32[128,256]{0,1:T(8,128)S(1)}, f32[128,256]{0,1:T(8,128)}, u32[]{:S(2)}) copy-start(f32[128,256]{0,1:T(8,128)} %copy.61) | copy-start | bytes 393220
  667.4 356.9 %copy-start.8 = (f32[128]{0:T(128)S(1)}, f32[128]{0:T(128)}, u32[]{:S(2)}) copy-start(f32[128]{0:T(128)} %copy-done.6) | copy-start | bytes 1540
  667.4 359.0 %copy-start.9 = (f32[2,128]{1,0:T(2,128)S(1)}, f32[2,128]{1,0:T(2,128)}, u32[]{:S(2)}) copy-start(f32[2,128]{1,0:T(2,128)} %get-tuple-element.405) | copy-start | bytes 3076
  667.4 359.0 %copy-start.11 = (f32[2,128]{1,0:T(2,128)S(1)}, f32[2,128]{1,0:T(2,128)}, u32[]{:S(2)}) copy-start(f32[2,128]{1,0:T(2,128)} %neg.22) | copy-start | bytes 3076
Sparse Core Ops, SparseCore 0:
  10.7 55.5 all-gather.9
  70.5 103.0 all-gather.11
  523.6 65.5 reduce-scatter.1
  593.8 87.6 all-gather.13
where the time goes:
time: 1040 us; the launch traced here: 1030 us
  other arithmetic  608 us (58%)
  blocking collectives  380 us (37%)
  matrix products  17.6 us (2%)
  between operations  15.9 us (2%)
  local copies, waits for them, and re-layouts  10.7 us (1%)
    unnamed x2, blocking collectives  273 us
    select_n x128, other arithmetic, entering_turn(): return jax.tree.map(lambda a, b: jnp.where(reached, a, b), new, before)  223 us
    select_n x126, other arithmetic, carried_turn(): jnp.where(position < mine, new, old)  221 us
    sub x64, other arithmetic, join_reverse(): keep = 1.0 - later[0]  79.6 us
    sub x63, other arithmetic, join_forward(): keep = 1.0 - later[0]  74.9 us
    all_gather x1, blocking collectives, carried_in(): pieces = jax.tree.map(lambda part: lax.all_gather(part, axis), value)  56.1 us
    all_gather x1, blocking collectives, entering(): lax.all_gather(part.astype(kind), axis)  51.4 us
  transfers between devices with their start and end apart: 4, of which 0 were waited for; matrix products, arithmetic and copies ran while one was open for 3% of the time, Pallas kernels for 0%

commit v1 on v0

v1 whole, which is shorter than its diff:
```python
import functools

import jax
import jax.numpy as jnp
from jax import lax
from jax.experimental import pallas as pl
from jax.experimental.pallas import tpu as pltpu
from jax.sharding import PartitionSpec as P

DH = 128
LENGTH = 128
WIDTH = 2 * DH
SMALL = 16
SCALE = DH ** (-0.5)
MESH = pl.DeviceIdType.MESH
F32, BF16 = jnp.float32, jnp.bfloat16


def dot(a, b, contract_a, contract_b):
    return lax.dot_general(
        a, b, (((contract_a,), (contract_b,)), ((), ())), preferred_element_type=F32
    )


def phi(x):
    return jnp.where(x > 0, x + 1.0, jnp.exp(jnp.minimum(x, 0.0)))


def phi_slope(x):
    return jnp.where(x > 0, 1.0, jnp.where(x == 0, 0.5, jnp.exp(jnp.minimum(x, 0.0))))


def both(one):
    return jnp.concatenate([one(slice(0, DH)), one(slice(DH, WIDTH))], axis=1)


def small_rows(norm, flag):
    high = norm.astype(BF16).astype(F32)
    at = lax.broadcasted_iota(jnp.int32, (SMALL, WIDTH), 0)
    rows = jnp.where(at == 0, high, jnp.where(at == 1, norm - high, jnp.where(at == 2, flag, 0.0)))
    return rows.astype(BF16)


def split_small(ref, place, rows):
    small = ref[place, rows : rows + SMALL, :].astype(F32)
    return small[0:1] + small[1:2], small[2:3]


class Scan:
    def __init__(self, me, sizes, reverse, msg1, buf1, msg2, buf2, msg3, carried, send, recv):
        self.me, self.sizes, self.reverse = me, sizes, reverse
        self.msg1, self.buf1, self.msg2, self.buf2 = msg1, buf1, msg2, buf2
        self.msg3, self.carried, self.send, self.recv = msg3, carried, send, recv
        self.rows = LENGTH // sizes[0]
        self.sent = []

    def copy(self, phase, j, src, dst, peer):
        one = pltpu.make_async_remote_copy(
            src_ref=src,
            dst_ref=dst,
            send_sem=self.send.at[phase, j],
            recv_sem=self.recv.at[phase, j],
            device_id=peer,
            device_id_type=MESH,
        )
        one.start()
        self.sent.append(one)
        return one

    def start(self, state, norm, flag):
        x = self.me["x"]
        small = small_rows(norm, flag)
        state = state.astype(BF16)
        for i in range(self.sizes[0]):
            self.msg1[i, 0 : self.rows, :] = state[i * self.rows : (i + 1) * self.rows]
            self.msg1[i, self.rows :, :] = small
        self.buf1[x] = self.msg1[x]

    def send_first(self):
        x, X = self.me["x"], self.sizes[0]
        self.first = []
        for j in range(1, X):
            to = lax.rem(x + j, X)
            self.first.append(
                self.copy(0, j, self.msg1.at[to], self.buf1.at[x], self.me["x_peer"](j))
            )

    def step(self, i, carry):
        acc, acc_norm, still_open = carry
        norm, flag = split_small(self.buf1, i, self.rows)
        block = self.buf1[i, 0 : self.rows, :].astype(F32)
        opened = 1.0 - flag
        if self.reverse:
            return acc, acc_norm, (
                opened * (acc + block),
                opened * (acc_norm + norm),
                still_open * opened,
            )
        acc, acc_norm = opened * acc, opened * acc_norm
        return acc, acc_norm, (acc + block, acc_norm + norm, still_open * opened)

    def order(self, n):
        return range(n - 1, -1, -1) if self.reverse else range(n)

    def second(self):
        for one in self.first:
            one.wait_recv()
        y, (X, Y) = self.me["y"], self.sizes
        carry = (
            jnp.zeros((self.rows, WIDTH), F32),
            jnp.zeros((1, WIDTH), F32),
            jnp.ones((1, WIDTH), F32),
        )
        for i in self.order(X):
            _, _, carry = self.step(i, carry)
        self.msg2[0 : self.rows, :] = carry[0].astype(BF16)
        self.msg2[self.rows :, :] = small_rows(carry[1], carry[2])
        self.buf2[y] = self.msg2[...]
        self.waits = [
            self.copy(1, j, self.msg2, self.buf2.at[y], self.me["y_peer"](j)) for j in range(1, Y)
        ]

    def third(self):
        for one in self.waits:
            one.wait_recv()
        x, y, (X, Y) = self.me["x"], self.me["y"], self.sizes
        acc, acc_norm = jnp.zeros((self.rows, WIDTH), F32), jnp.zeros((1, WIDTH), F32)
        at = jnp.full((1, WIDTH), y, jnp.int32)
        for i in self.order(Y):
            norm, still_open = split_small(self.buf2, i, self.rows)
            block = self.buf2[i, 0 : self.rows, :].astype(F32)
            counts = jnp.where((at < i) if self.reverse else (at > i), 1.0, 0.0)
            acc = counts * (block + still_open * acc) + (1.0 - counts) * acc
            acc_norm = counts * (norm + still_open * acc_norm) + (1.0 - counts) * acc_norm
        carry = (acc, acc_norm, jnp.ones((1, WIDTH), F32))
        mine = jnp.zeros((1, WIDTH), F32)
        at = jnp.full((1, WIDTH), x, jnp.int32)
        for i in self.order(X):
            enters, enters_norm, carry = self.step(i, carry)
            self.msg3[i] = enters.astype(BF16)
            mine = jnp.where(at == i, enters_norm, mine)
        here = pl.ds(pl.multiple_of(x * self.rows, self.rows), self.rows)
        self.carried[here, :] = self.msg3[x]
        self.waits = []
        for j in range(1, X):
            to = lax.rem(x + j, X)
            self.waits.append(
                self.copy(2, j, self.msg3.at[to], self.carried.at[here, :], self.me["x_peer"](j))
            )
        return mine

    def finish(self):
        for one in self.waits:
            one.wait_recv()
        return self.carried[...]


def layer(
    sizes,
    gate_ref,
    valid_ref,
    starts_ref,
    q_hbm,
    k_hbm,
    v_hbm,
    og_hbm,
    w_hbm,
    out_hbm,
    dq_hbm,
    dk_hbm,
    dv_hbm,
    q_ref,
    k_ref,
    v_ref,
    og_all,
    w_ref,
    w_other,
    results,
    probs_ref,
    local_ref,
    sigq_ref,
    read_ref,
    mixed_ref,
    mixed_other,
    rs_send,
    rs_recv,
    f_msg1,
    f_buf1,
    f_msg2,
    f_buf2,
    f_msg3,
    f_in,
    b_msg1,
    b_buf1,
    b_msg2,
    b_buf2,
    b_msg3,
    b_in,
    load_sem,
    store_sem,
    f_send,
    f_recv,
    b_send,
    b_recv,
    ag_send,
    ag_recv,
    fw_send,
    fw_recv,
    w_send,
    w_recv,
    mix_send,
    mix_recv,
    r_send,
    r_recv,
):
    X, Y, Z = sizes
    seq, head = lax.axis_index("seq"), lax.axis_index("head")
    y, x = lax.div(seq, X), lax.rem(seq, X)
    z, core = lax.div(head, 2), lax.rem(head, 2)

    def x_peer(j):
        return (y * X + lax.rem(x + j, X), head)

    def y_peer(j):
        return (lax.rem(y + j, Y) * X + x, head)

    def z_peer(j):
        return (seq, lax.rem(z + j, Z) * 2 + core)

    partner = (seq, z * 2 + (1 - core))
    me = {"x": x, "y": y, "x_peer": x_peer, "y_peer": y_peer}
    sent = []

    def remote(src, dst, send, recv, peer):
        one = pltpu.make_async_remote_copy(
            src_ref=src,
            dst_ref=dst,
            send_sem=send,
            recv_sem=recv,
            device_id=peer,
            device_id_type=MESH,
        )
        one.start()
        sent.append(one)
        return one

    loads = {}
    for n, (name, src, dst) in enumerate(
        (
            ("k", k_hbm, k_ref),
            ("v", v_hbm, v_ref),
            ("og", og_hbm, og_all.at[head]),
            ("q", q_hbm, q_ref),
            ("w", w_hbm, w_ref),
        )
    ):
        loads[name] = pltpu.make_async_copy(src, dst, load_sem.at[n])
        loads[name].start()

    barrier = pltpu.get_barrier_semaphore()
    peers = [x_peer(j) for j in range(1, X)] + [y_peer(j) for j in range(1, Y)]
    peers += [z_peer(j) for j in range(1, Z)] + [partner]
    for peer in peers:
        pl.semaphore_signal(barrier, inc=1, device_id=peer, device_id_type=MESH)

    forward = Scan(
        me, (X, Y), False, f_msg1, f_buf1, f_msg2, f_buf2, f_msg3, f_in, f_send, f_recv
    )
    backward = Scan(
        me, (X, Y), True, b_msg1, b_buf1, b_msg2, b_buf2, b_msg3, b_in, b_send, b_recv
    )

    live = lax.broadcasted_iota(jnp.int32, (LENGTH, WIDTH), 0) < valid_ref[0]
    flag = jnp.full((1, WIDTH), starts_ref[0], jnp.int32).astype(F32)
    lanes = lax.broadcasted_iota(jnp.int32, (1, WIDTH), 1)
    logit = jnp.where(
        lanes < DH, jnp.full((1, WIDTH), gate_ref[0], F32), jnp.full((1, WIDTH), gate_ref[1], F32)
    )
    gate = 1.0 / (1.0 + jnp.exp(-logit))

    loads["k"].wait()
    loads["v"].wait()
    sigk = jnp.where(live, phi(k_ref[...].astype(F32)), 0.0)
    sigk_low = sigk.astype(BF16)
    v_low = v_ref[...]
    state = both(lambda h: dot(sigk_low[:, h], v_low[:, h], 0, 0))
    forward.start(state, jnp.sum(sigk, axis=0, keepdims=True), flag)

    pl.semaphore_wait(barrier, len(peers))
    forward.send_first()

    loads["og"].wait()
    gathers = [
        remote(og_all.at[head], og_all.at[head], ag_send.at[j], ag_recv.at[j], z_peer(j))
        for j in range(1, Z)
    ]
    passed = [remote(og_all.at[head], og_all.at[head], fw_send.at[0], fw_recv.at[0], partner)]
    weights = []
    for i in range(Z):
        columns = pl.ds(pl.multiple_of((2 * i + 1 - core) * WIDTH, WIDTH), WIDTH)
        weights.append(
            remote(w_hbm.at[:, columns], w_other.at[i], w_send.at[i], w_recv.at[i], partner)
        )

    loads["q"].wait()
    row = lax.broadcasted_iota(jnp.int32, (LENGTH, LENGTH), 0)
    col = lax.broadcasted_iota(jnp.int32, (LENGTH, LENGTH), 1)
    allowed = (col <= row) & (col < valid_ref[0])
    for n in range(2):
        h = slice(n * DH, (n + 1) * DH)
        scores = dot(q_ref[:, h], k_ref[:, h], 1, 1) * SCALE
        scores = jnp.where(allowed, scores, -1e30)
        expo = jnp.exp(scores - jnp.max(scores, axis=1, keepdims=True))
        probs = expo / jnp.sum(expo, axis=1, keepdims=True)
        probs_ref[n] = probs
        local_ref[:, h] = dot(probs.astype(BF16), v_ref[:, h], 1, 0)

    forward.second()
    sigq = phi(q_ref[...].astype(F32))
    sigq_ref[...] = sigq.astype(BF16)
    norm_in = forward.third()

    def pass_on(j):
        gathers[j - 1].wait_recv()
        block = og_all.at[lax.rem(z - j + Z, Z) * 2 + core]
        passed.append(remote(block, block, fw_send.at[j], fw_recv.at[j], partner))

    scaled = sigq * norm_in
    inverse = both(
        lambda h: jnp.broadcast_to(
            1.0 / (jnp.sum(scaled[:, h], axis=1, keepdims=True) + 1.0), (LENGTH, DH)
        )
    )

    mem_in = forward.finish()
    read = both(lambda h: dot(sigq_ref[:, h], mem_in[:, h], 1, 0)) * inverse
    read_ref[...] = read
    mixed = jnp.where(live, gate * read + (1.0 - gate) * local_ref[...], 0.0)
    mixed_ref[...] = mixed.astype(BF16)
    mixing = remote(mixed_ref, mixed_other, mix_send.at[0], mix_recv.at[0], partner)

    near_first = sorted(range(1, Z), key=lambda j: min(j, Z - j))
    for j in near_first:
        pass_on(j)

    loads["w"].wait()
    for one in weights:
        one.wait_recv()
    mixing.wait_recv()

    def part(target):
        columns = pl.ds(pl.multiple_of((2 * target + core) * WIDTH, WIDTH), WIDTH)
        return dot(mixed_ref[...], w_ref[:, columns], 1, 0) + dot(
            mixed_other[...], w_other[target], 1, 0
        )

    reduces = []
    for j in reversed(near_first):
        rs_send[j] = part(lax.rem(z + j, Z)).astype(BF16)
        reduces.append(
            remote(rs_send.at[j], rs_recv.at[j], r_send.at[j], r_recv.at[j], z_peer(j))
        )

    for one in passed:
        one.wait_recv()
    grad = jnp.zeros((LENGTH, WIDTH), F32)
    for i in range(2 * Z):
        grad = grad + dot(og_all[i], w_ref[:, i * WIDTH : (i + 1) * WIDTH], 1, 1)
    grad = jnp.where(live, grad.astype(BF16).astype(F32), 0.0)
    read_grad = gate * grad
    local_grad = ((1.0 - gate) * grad).astype(BF16)
    numer_grad = (read_grad * inverse).astype(BF16)
    product = read_grad * read_ref[...]
    denom_grad = -inverse * both(
        lambda h: jnp.broadcast_to(jnp.sum(product[:, h], axis=1, keepdims=True), (LENGTH, DH))
    )
    state_grad = both(lambda h: dot(sigq_ref[:, h], numer_grad[:, h], 0, 0))
    norm_grad = jnp.sum(phi(q_ref[...].astype(F32)) * denom_grad, axis=0, keepdims=True)
    backward.start(state_grad, norm_grad, flag)
    backward.send_first()

    parts = []
    for n in range(2):
        h = slice(n * DH, (n + 1) * DH)
        probs = probs_ref[n]
        probs_grad = dot(local_grad[:, h], v_ref[:, h], 1, 1)
        inner = jnp.sum(probs_grad * probs, axis=1, keepdims=True)
        scores_grad = (probs * (probs_grad - inner) * SCALE).astype(BF16)
        parts.append(
            (
                dot(scores_grad, k_ref[:, h], 1, 0)
                + (dot(numer_grad[:, h], f_in[:, h], 1, 1) + denom_grad[:, h] * norm_in[:, h])
                * phi_slope(q_ref[:, h].astype(F32)),
                dot(scores_grad, q_ref[:, h], 0, 0),
                dot(probs.astype(BF16), local_grad[:, h], 0, 0),
            )
        )
    stores = []

    def store(n, value, target):
        results[n] = value.astype(BF16)
        one = pltpu.make_async_copy(results.at[n], target, store_sem.at[n])
        one.start()
        stores.append(one)

    store(1, jnp.concatenate([parts[0][0], parts[1][0]], axis=1), dq_hbm)
    key_part = jnp.concatenate([parts[0][1], parts[1][1]], axis=1)
    value_part = jnp.concatenate([parts[0][2], parts[1][2]], axis=1)
    own = part(z)

    backward.second()
    norm_back = backward.third()
    mem_back = backward.finish()
    k_float = k_ref[...].astype(F32)
    key_more = (both(lambda h: dot(v_ref[:, h], mem_back[:, h], 1, 1)) + norm_back) * phi_slope(
        k_float
    )
    store(2, key_part + jnp.where(live, key_more, 0.0), dk_hbm)
    sigk_low = jnp.where(live, phi(k_float), 0.0).astype(BF16)
    store(3, value_part + both(lambda h: dot(sigk_low[:, h], mem_back[:, h], 1, 0)), dv_hbm)

    total = own
    for j, one in zip(reversed(near_first), reduces):
        one.wait_recv()
        total = total + rs_recv[j].astype(F32)
    store(0, total, out_hbm)

    for one in sent + forward.sent + backward.sent:
        one.wait_send()
    for one in stores:
        one.wait()


def build(mesh, X):
    Y, Z = mesh.shape["seq"] // X, mesh.shape["head"] // 2
    rows = LENGTH // X
    dma = pltpu.SemaphoreType.DMA

    def scan_scratch():
        return [
            pltpu.VMEM((X, rows + SMALL, WIDTH), BF16),
            pltpu.VMEM((X, rows + SMALL, WIDTH), BF16),
            pltpu.VMEM((rows + SMALL, WIDTH), BF16),
            pltpu.VMEM((Y, rows + SMALL, WIDTH), BF16),
            pltpu.VMEM((X, rows, WIDTH), BF16),
            pltpu.VMEM((LENGTH, WIDTH), BF16),
        ]

    def block():
        return pltpu.VMEM((LENGTH, WIDTH), BF16)

    def wide():
        return pltpu.VMEM((LENGTH, WIDTH), F32)

    most = max(X, Y)
    scratch = [
        block(),
        block(),
        block(),
        pltpu.VMEM((2 * Z, LENGTH, WIDTH), BF16),
        pltpu.VMEM((WIDTH, 2 * Z * WIDTH), BF16),
        pltpu.VMEM((Z, WIDTH, WIDTH), BF16),
        pltpu.VMEM((4, LENGTH, WIDTH), BF16),
        pltpu.VMEM((2, LENGTH, LENGTH), F32),
        wide(),
        block(),
        wide(),
        block(),
        block(),
        pltpu.VMEM((Z, LENGTH, WIDTH), BF16),
        pltpu.VMEM((Z, LENGTH, WIDTH), BF16),
        *scan_scratch(),
        *scan_scratch(),
        dma((5,)),
        dma((4,)),
        dma((3, most)),
        dma((3, most)),
        dma((3, most)),
        dma((3, most)),
        dma((Z,)),
        dma((Z,)),
        dma((Z,)),
        dma((Z,)),
        dma((Z,)),
        dma((Z,)),
        dma((1,)),
        dma((1,)),
        dma((Z,)),
        dma((Z,)),
    ]

    def shards(queries, keys, values, gate, out_weight, out_grad, valid, starts):
        one = jax.ShapeDtypeStruct((LENGTH, WIDTH), BF16)
        return pl.pallas_call(
            functools.partial(layer, (X, Y, Z)),
            out_shape=(one,) * 4,
            in_specs=[pl.BlockSpec(memory_space=pltpu.SMEM)] * 3
            + [pl.BlockSpec(memory_space=pl.ANY)] * 5,
            out_specs=(pl.BlockSpec(memory_space=pl.ANY),) * 4,
            scratch_shapes=scratch,
            compiler_params=pltpu.CompilerParams(
                collective_id=0, has_side_effects=True, vmem_limit_bytes=40 * 1024 * 1024
            ),
            name="layer",
        )(gate, valid, starts, queries, keys, values, out_grad, out_weight)

    placed = (
        P("seq", "head"),
        P("seq", "head"),
        P("seq", "head"),
        P("head"),
        P("head", None),
        P("seq", "head"),
        P("seq"),
        P("seq"),
    )
    return jax.shard_map(
        shards, mesh=mesh, in_specs=placed, out_specs=(P("seq", "head"),) * 4, check_vma=False
    )


def solution(mesh):
    return build(mesh, 8)
```

time: 1040 us -> 70.3 us (0.07)
  the two profiles are of different devices: /device:TPU:14 before, /device:TPU:1 now
where the time goes in v1:
time: 70.3 us; the launch traced here: 69.9 us
  Pallas kernels  59.8 us (85%)
  local copies, waits for them, and re-layouts  8.11 us (12%)
  between operations  1.95 us (3%)
    pallas_call x1, Pallas kernels, shards(): pl.pallas_call(functools.partial(layer, (X, Y, Z)), out_shape=(one,) * 4,...  59.8 us
    unnamed x16, local copies, waits for them, and re-layouts  8.11 us

profile of v1, /device:TPU:1, one launch (start us, length us, event | category | flops | bytes accessed | tf_op | source)
XLA Modules:
  0.0 69.9 jit_solution(2179017851214846239)
XLA Ops:
  1.9 0.0 copy-start
  1.9 1.6 %copy-done = bf16[256,4096]{1,0:T(8,128)(2,1)S(1)} copy-done((bf16[256,4096]{1,0:T(8,128)(2,1)S(1)}, bf16[256,4096]{1,0:T(8,128)(2,1)}, u32[]{:S(2)}) %copy-start) | copy-done | bytes 2097176
  3.5 0.0 copy-start.1
  3.5 0.8 %copy-done.1 = bf16[128,256]{1,0:T(8,128)(2,1)S(1)} copy-done((bf16[128,256]{1,0:T(8,128)(2,1)S(1)}, bf16[128,256]{1,0:T(8,128)(2,1)}, u32[]{:S(2)}) %copy-start.1) | copy-done | bytes 65560
  4.4 0.0 copy-start.2
  4.4 0.8 %copy-done.2 = bf16[128,256]{1,0:T(8,128)(2,1)S(1)} copy-done((bf16[128,256]{1,0:T(8,128)(2,1)S(1)}, bf16[128,256]{1,0:T(8,128)(2,1)}, u32[]{:S(2)}) %copy-start.2) | copy-done | bytes 65560
  5.2 0.0 copy-start.3
  5.2 0.8 %copy-done.3 = bf16[128,256]{1,0:T(8,128)(2,1)S(1)} copy-done((bf16[128,256]{1,0:T(8,128)(2,1)S(1)}, bf16[128,256]{1,0:T(8,128)(2,1)}, u32[]{:S(2)}) %copy-start.3) | copy-done | bytes 65560
  6.0 0.0 copy-start.4
  6.0 0.8 %copy-done.4 = bf16[128,256]{1,0:T(8,128)(2,1)S(1)} copy-done((bf16[128,256]{1,0:T(8,128)(2,1)S(1)}, bf16[128,256]{1,0:T(8,128)(2,1)}, u32[]{:S(2)}) %copy-start.4) | copy-done | bytes 65560
  6.9 0.0 copy-start.5
  6.9 0.7 copy-done.5
  7.5 59.8 %layer.1 = (bf16[128,256]{1,0:T(8,128)(2,1)S(1)}, bf16[128,256]{1,0:T(8,128)(2,1)S(1)}, bf16[128,256]{1,0:T(8,128)(2,1)S(1)}, bf16[128,256]{1,0:T(8,128)(2,1)S(1)}) custom-call(f32[2]{0:T(128)S(1)} %copy-done.5, s32[1]{0:T(128)S(6)} %copy.16.valid_ref, s32[1]{0:T(128)S(6)} %copy.17.starts_ref, bf16[128,256]{1,0:T(8,128)(2,1)S(1)} %copy-done.1, ...), custom_call_target="tpu_custom_call" | custom-call | tf_op jit(solution)/shard_map/layer/pallas_call | solution.py:494
  67.4 0.6 copy.18
  68.0 0.6 copy.19
  68.6 0.6 copy.20
  69.3 0.6 copy.21
Async XLA Ops:
  1.9 1.6 %copy-start = (bf16[256,4096]{1,0:T(8,128)(2,1)S(1)}, bf16[256,4096]{1,0:T(8,128)(2,1)}, u32[]{:S(2)}) copy-start(bf16[256,4096]{1,0:T(8,128)(2,1)} %w_hbm.1) | copy-start | bytes 6291460
  3.5 0.8 %copy-start.1 = (bf16[128,256]{1,0:T(8,128)(2,1)S(1)}, bf16[128,256]{1,0:T(8,128)(2,1)}, u32[]{:S(2)}) copy-start(bf16[128,256]{1,0:T(8,128)(2,1)} %q_hbm.1) | copy-start | bytes 196612
  4.4 0.8 %copy-start.2 = (bf16[128,256]{1,0:T(8,128)(2,1)S(1)}, bf16[128,256]{1,0:T(8,128)(2,1)}, u32[]{:S(2)}) copy-start(bf16[128,256]{1,0:T(8,128)(2,1)} %k_hbm.1) | copy-start | bytes 196612
  5.2 0.8 %copy-start.3 = (bf16[128,256]{1,0:T(8,128)(2,1)S(1)}, bf16[128,256]{1,0:T(8,128)(2,1)}, u32[]{:S(2)}) copy-start(bf16[128,256]{1,0:T(8,128)(2,1)} %v_hbm.1) | copy-start | bytes 196612
  6.0 0.8 %copy-start.4 = (bf16[128,256]{1,0:T(8,128)(2,1)S(1)}, bf16[128,256]{1,0:T(8,128)(2,1)}, u32[]{:S(2)}) copy-start(bf16[128,256]{1,0:T(8,128)(2,1)} %og_hbm.1) | copy-start | bytes 196612
  6.9 0.7 copy-start.5

commit v2 on v1

--- a/solution.py
+++ b/solution.py
@@ -157,9 +157,9 @@
 
 def layer(
     sizes,
-    gate_ref,
-    valid_ref,
-    starts_ref,
+    gate_hbm,
+    valid_hbm,
+    starts_hbm,
     q_hbm,
     k_hbm,
     v_hbm,
@@ -169,6 +169,9 @@
     dq_hbm,
     dk_hbm,
     dv_hbm,
+    gate_ref,
+    valid_ref,
+    starts_ref,
     q_ref,
     k_ref,
     v_ref,
@@ -247,6 +250,9 @@
     loads = {}
     for n, (name, src, dst) in enumerate(
         (
+            ("valid", valid_hbm, valid_ref),
+            ("starts", starts_hbm, starts_ref),
+            ("gate", gate_hbm, gate_ref),
             ("k", k_hbm, k_ref),
             ("v", v_hbm, v_ref),
             ("og", og_hbm, og_all.at[head]),
@@ -270,6 +276,8 @@
         me, (X, Y), True, b_msg1, b_buf1, b_msg2, b_buf2, b_msg3, b_in, b_send, b_recv
     )
 
+    for name in ("valid", "starts", "gate"):
+        loads[name].wait()
     live = lax.broadcasted_iota(jnp.int32, (LENGTH, WIDTH), 0) < valid_ref[0]
     flag = jnp.full((1, WIDTH), starts_ref[0], jnp.int32).astype(F32)
     lanes = lax.broadcasted_iota(jnp.int32, (1, WIDTH), 1)
@@ -431,6 +439,19 @@
         one.wait()
 
 
+def store_all(*refs):
+    sources, targets, held, sem = refs[:4], refs[4:8], refs[8], refs[9]
+    loads = [pltpu.make_async_copy(sources[n], held.at[n], sem.at[0, n]) for n in range(4)]
+    stores = [pltpu.make_async_copy(held.at[n], targets[n], sem.at[1, n]) for n in range(4)]
+    for one in loads:
+        one.start()
+    for load, one in zip(loads, stores):
+        load.wait()
+        one.start()
+    for one in stores:
+        one.wait()
+
+
 def build(mesh, X):
     Y, Z = mesh.shape["seq"] // X, mesh.shape["head"] // 2
     rows = LENGTH // X
@@ -454,6 +475,9 @@
 
     most = max(X, Y)
     scratch = [
+        pltpu.SMEM((2,), F32),
+        pltpu.SMEM((1,), jnp.int32),
+        pltpu.SMEM((1,), jnp.int32),
         block(),
         block(),
         block(),
@@ -471,7 +495,7 @@
         pltpu.VMEM((Z, LENGTH, WIDTH), BF16),
         *scan_scratch(),
         *scan_scratch(),
-        dma((5,)),
+        dma((8,)),
         dma((4,)),
         dma((3, most)),
         dma((3, most)),
@@ -491,18 +515,26 @@
 
     def shards(queries, keys, values, gate, out_weight, out_grad, valid, starts):
         one = jax.ShapeDtypeStruct((LENGTH, WIDTH), BF16)
-        return pl.pallas_call(
+        results = pl.pallas_call(
             functools.partial(layer, (X, Y, Z)),
             out_shape=(one,) * 4,
-            in_specs=[pl.BlockSpec(memory_space=pltpu.SMEM)] * 3
-            + [pl.BlockSpec(memory_space=pl.ANY)] * 5,
+            in_specs=[pl.BlockSpec(memory_space=pltpu.HBM)] * 8,
             out_specs=(pl.BlockSpec(memory_space=pl.ANY),) * 4,
             scratch_shapes=scratch,
             compiler_params=pltpu.CompilerParams(
-                collective_id=0, has_side_effects=True, vmem_limit_bytes=40 * 1024 * 1024
+                collective_id=0, has_side_effects=True, vmem_limit_bytes=63 * 1024 * 1024
             ),
             name="layer",
         )(gate, valid, starts, queries, keys, values, out_grad, out_weight)
+        return pl.pallas_call(
+            store_all,
+            out_shape=(one,) * 4,
+            in_specs=[pl.BlockSpec(memory_space=pl.ANY)] * 4,
+            out_specs=(pl.BlockSpec(memory_space=pltpu.HBM),) * 4,
+            scratch_shapes=[pltpu.VMEM((4, LENGTH, WIDTH), BF16), dma((2, 4))],
+            compiler_params=pltpu.CompilerParams(vmem_limit_bytes=63 * 1024 * 1024),
+            name="store_all",
+        )(*results)
 
     placed = (
         P("seq", "head"),

time: 70.3 us -> 62.7 us (0.89)
  local copies, waits for them, and re-layouts: 8.11 us -> 0 us
  Pallas kernels: 59.8 us -> 60.6 us
    unnamed x16 -> x0, local copies, waits for them, and re-layouts: 8.11 us -> none
    pallas_call x0 -> x1, Pallas kernels: none -> 1.63 us  [shards(): pl.pallas_call(store_all, out_shape=(one,) * 4, in_specs=[pl.BlockSpec(me...]
    pallas_call x1, Pallas kernels: 59.8 us -> 58.9 us  [shards(): pl.pallas_call(functools.partial(layer, (X, Y, Z)), out_shape=(one,) * 4,...]
where the time goes in v2:
time: 62.7 us; the launch traced here: 62.5 us
  Pallas kernels  60.6 us (97%)
  between operations  1.93 us (3%)
    pallas_call x1, Pallas kernels, shards(): pl.pallas_call(functools.partial(layer, (X, Y, Z)), out_shape=(one,) * 4,...  58.9 us
    pallas_call x1, Pallas kernels, shards(): pl.pallas_call(store_all, out_shape=(one,) * 4, in_specs=[pl.BlockSpec(me...  1.63 us

profile of v2, /device:TPU:1, one launch (start us, length us, event | category | flops | bytes accessed | tf_op | source)
XLA Modules:
  0.0 62.5 jit_solution(13292935463367310750)
XLA Ops:
  1.9 58.9 %layer.1 = (bf16[128,256]{1,0:T(8,128)(2,1)}, bf16[128,256]{1,0:T(8,128)(2,1)}, bf16[128,256]{1,0:T(8,128)(2,1)}, bf16[128,256]{1,0:T(8,128)(2,1)}) custom-call(f32[2]{0:T(128)} %gate_hbm.1, s32[1]{0:T(128)S(6)} %copy.12.valid_hbm, s32[1]{0:T(128)S(6)} %copy.13.starts_hbm, bf16[128,256]{1,0:T(8,128)(2,1)} %q_hbm.1, bf16[128,256]{1,0:T(8,128)(2,1)} %k_hbm.1, ...), custom_call_target="tpu_custom_call" | custom-call | tf_op jit(solution)/shard_map/layer/pallas_call | solution.py:518
  60.9 1.6 %store_all.1 = (bf16[128,256]{1,0:T(8,128)(2,1)}, bf16[128,256]{1,0:T(8,128)(2,1)}, bf16[128,256]{1,0:T(8,128)(2,1)}, bf16[128,256]{1,0:T(8,128)(2,1)}) custom-call(bf16[128,256]{1,0:T(8,128)(2,1)} %get-tuple-element.8.refs_0_, bf16[128,256]{1,0:T(8,128)(2,1)} %get-tuple-element.9.refs_1_, bf16[128,256]{1,0:T(8,128)(2,1)} %get-tuple-element.10.refs_2_, ...), custom_call_target="tpu_custom_call" | custom-call | tf_op jit(solution)/shard_map/store_all/pallas_call | solution.py:529

commit v3 on v2

v3 whole, which is shorter than its diff:
```python
import functools

import jax
import jax.numpy as jnp
from jax import lax
from jax.experimental import pallas as pl
from jax.experimental.pallas import tpu as pltpu
from jax.sharding import PartitionSpec as P

DH = 128
LENGTH = 128
WIDTH = 2 * DH
SMALL = 16
SCALE = DH ** (-0.5)
MESH = pl.DeviceIdType.MESH
F32, BF16 = jnp.float32, jnp.bfloat16


def dot(a, b, contract_a, contract_b):
    return lax.dot_general(
        a, b, (((contract_a,), (contract_b,)), ((), ())), preferred_element_type=F32
    )


def phi(x):
    return jnp.where(x > 0, x + 1.0, jnp.exp(jnp.minimum(x, 0.0)))


def phi_slope(x):
    return jnp.where(x > 0, 1.0, jnp.where(x == 0, 0.5, jnp.exp(jnp.minimum(x, 0.0))))


def both(one):
    return jnp.concatenate([one(slice(0, DH)), one(slice(DH, WIDTH))], axis=1)


def small_rows(norm, flag):
    high = norm.astype(BF16).astype(F32)
    low = norm - high
    at = lax.broadcasted_iota(jnp.int32, (SMALL, DH), 0)
    rows = jnp.zeros((SMALL, DH), F32)
    for n, row in enumerate(
        (high[:, :DH], high[:, DH:], low[:, :DH], low[:, DH:], flag[:, :DH])
    ):
        rows = jnp.where(at == n, row, rows)
    return rows.astype(BF16)


def split_small(small):
    small = small.astype(F32)
    norm = jnp.concatenate([small[0:1] + small[2:3], small[1:2] + small[3:4]], axis=1)
    return norm, jnp.concatenate([small[4:5], small[4:5]], axis=1)


def layer(
    sizes,
    gate_hbm,
    valid_hbm,
    starts_hbm,
    q_hbm,
    k_hbm,
    v_hbm,
    og_hbm,
    w_hbm,
    out_hbm,
    dq_hbm,
    dk_hbm,
    dv_hbm,
    gate_ref,
    valid_ref,
    starts_ref,
    q_ref,
    k_ref,
    v_ref,
    og_all,
    w_ref,
    w_other,
    results,
    probs_ref,
    local_ref,
    sigq_ref,
    read_ref,
    mixed_ref,
    mixed_other,
    grad_theirs,
    grad_other,
    part_ref,
    rs_send,
    rs_recv,
    f_msg1,
    f_buf1,
    f_msg2,
    f_buf2,
    f_msg3,
    f_in,
    b_msg1,
    b_buf1,
    b_msg2,
    b_buf2,
    b_msg3,
    b_in,
    n_msg1,
    n_buf1,
    n_msg2,
    n_buf2,
    load_sem,
    store_sem,
    scan_send,
    scan_recv,
    ag_send,
    ag_recv,
    w_send,
    w_recv,
    swap_send,
    swap_recv,
    rs_send_sem,
    rs_recv_sem,
):
    X, Y, Z = sizes
    rows = LENGTH // X
    half = LENGTH // 2
    seq, head = lax.axis_index("seq"), lax.axis_index("head")
    y, x = lax.div(seq, X), lax.rem(seq, X)
    z, core = lax.div(head, 2), lax.rem(head, 2)

    def x_peer(j):
        return (y * X + lax.rem(x + j, X), head)

    def y_peer(j):
        return (lax.rem(y + j, Y) * X + x, head)

    def z_at(j):
        return lax.rem(z + j + Z, Z)

    def z_peer(j):
        return (seq, z_at(j) * 2 + core)

    partner = (seq, z * 2 + (1 - core))
    sent = []

    def remote(src, dst, send, recv, peer):
        one = pltpu.make_async_remote_copy(
            src_ref=src,
            dst_ref=dst,
            send_sem=send,
            recv_sem=recv,
            device_id=peer,
            device_id_type=MESH,
        )
        one.start()
        sent.append(one)
        return one

    loads = {}
    for n, (name, src, dst) in enumerate(
        (
            ("og", og_hbm, og_all.at[z]),
            ("k", k_hbm, k_ref),
            ("v", v_hbm, v_ref),
            ("valid", valid_hbm, valid_ref),
            ("starts", starts_hbm, starts_ref),
            ("gate", gate_hbm, gate_ref),
            ("q", q_hbm, q_ref),
            ("w", w_hbm, w_ref),
        )
    ):
        loads[name] = pltpu.make_async_copy(src, dst, load_sem.at[n])
        loads[name].start()

    barrier = pltpu.get_barrier_semaphore()
    peers = [x_peer(j) for j in range(1, X)] + [y_peer(j) for j in range(1, Y)]
    relayed = Z == 8
    straight = (2, 6, 1, 7) if relayed else tuple(range(1, Z))
    peers += [z_peer(j) for j in straight] + [partner]
    for peer in peers:
        pl.semaphore_signal(barrier, inc=1, device_id=peer, device_id_type=MESH)

    def along_x(phase, source, target):
        return [
            remote(
                source(lax.rem(x + j, X)),
                target,
                scan_send.at[phase, j],
                scan_recv.at[phase, j],
                x_peer(j),
            )
            for j in range(1, X)
        ]

    def along_y(phase, source, target):
        return [
            remote(source, target, scan_send.at[phase, j], scan_recv.at[phase, j], y_peer(j))
            for j in range(1, Y)
        ]

    def arrived(copies):
        for one in copies:
            one.wait_recv()

    def pack(ref, place, block):
        ref[place, 0:rows, :] = block[:, :DH]
        ref[place, rows : 2 * rows, :] = block[:, DH:]

    def unpack(ref, place):
        return jnp.concatenate(
            [ref[place, 0:rows, :], ref[place, rows : 2 * rows, :]], axis=1
        ).astype(F32)

    def small_of(ref, place):
        return split_small(ref[place, 2 * rows : 2 * rows + SMALL, :])

    zero_block, zero_row = jnp.zeros((rows, WIDTH), F32), jnp.zeros((1, WIDTH), F32)
    x_row, y_row = jnp.full((1, WIDTH), x, jnp.int32), jnp.full((1, WIDTH), y, jnp.int32)
    here = pl.ds(pl.multiple_of(x * rows, rows), rows)

    upper, lower, full = slice(0, half), slice(half, LENGTH), slice(0, LENGTH)

    def gather(n, block, part, to):
        piece = og_all.at[z_at(block), part]
        return remote(piece, piece, ag_send.at[n], ag_recv.at[n], z_peer(to))

    pl.semaphore_wait(barrier, len(peers))
    loads["og"].wait()
    gathers = {n: gather(n, 0, full, to) for n, to in enumerate(straight)}

    for name in ("valid", "starts", "gate"):
        loads[name].wait()
    live = lax.broadcasted_iota(jnp.int32, (LENGTH, WIDTH), 0) < valid_ref[0]
    flag = jnp.full((1, WIDTH), starts_ref[0], jnp.int32).astype(F32)
    lanes = lax.broadcasted_iota(jnp.int32, (1, WIDTH), 1)
    logit = jnp.where(
        lanes < DH, jnp.full((1, WIDTH), gate_ref[0], F32), jnp.full((1, WIDTH), gate_ref[1], F32)
    )
    gate = 1.0 / (1.0 + jnp.exp(-logit))

    loads["k"].wait()
    sigk = jnp.where(live, phi(k_ref[...].astype(F32)), 0.0)
    sigk_low = sigk.astype(BF16)
    loads["v"].wait()
    state = both(lambda h: dot(sigk_low[:, h], v_ref[:, h], 0, 0)).astype(BF16)
    small = small_rows(jnp.sum(sigk, axis=0, keepdims=True), flag)
    for i in range(X):
        pack(f_msg1, i, state[i * rows : (i + 1) * rows])
        f_msg1[i, 2 * rows :, :] = small
    f_buf1[x] = f_msg1[x]

    first = along_x(0, lambda to: f_msg1.at[to], f_buf1.at[x])

    weights = []
    for i in range(Z):
        columns = pl.ds(pl.multiple_of((2 * i + 1 - core) * WIDTH, WIDTH), WIDTH)
        weights.append(
            remote(w_hbm.at[:, columns], w_other.at[i], w_send.at[i], w_recv.at[i], partner)
        )

    loads["q"].wait()
    row = lax.broadcasted_iota(jnp.int32, (LENGTH, LENGTH), 0)
    col = lax.broadcasted_iota(jnp.int32, (LENGTH, LENGTH), 1)
    allowed = (col <= row) & (col < valid_ref[0])
    for n in range(2):
        h = slice(n * DH, (n + 1) * DH)
        scores = dot(q_ref[:, h], k_ref[:, h], 1, 1) * SCALE
        scores = jnp.where(allowed, scores, -1e30)
        expo = jnp.exp(scores - jnp.max(scores, axis=1, keepdims=True))
        probs = expo / jnp.sum(expo, axis=1, keepdims=True)
        probs_ref[n] = probs
        local_ref[:, h] = dot(probs.astype(BF16), v_ref[:, h], 1, 0)

    if relayed:
        for n, (came, block, part, to) in enumerate(
            ((0, -2, upper, 2), (0, -2, full, 1), (1, 2, lower, -2), (1, 2, full, -1))
        ):
            if n % 2 == 0:
                gathers[came].wait_recv()
            gathers[4 + n] = gather(4 + n, block, part, to)

    arrived(first)
    acc, acc_norm, still_open = zero_block, zero_row, jnp.ones((1, WIDTH), F32)
    for i in range(X):
        norm, start = small_of(f_buf1, i)
        opened = 1.0 - start
        acc = opened * acc + unpack(f_buf1, i)
        acc_norm = opened * acc_norm + norm
        still_open = still_open * opened
    pack(f_msg2, 0, acc.astype(BF16))
    f_msg2[0, 2 * rows :, :] = small_rows(acc_norm, still_open)
    f_buf2[y] = f_msg2[0]
    second = along_y(1, f_msg2.at[0], f_buf2.at[y])

    sigq = phi(q_ref[...].astype(F32))
    sigq_ref[...] = sigq.astype(BF16)

    def cotangent(j):
        block = z_at(j)
        columns = pl.ds(pl.multiple_of((2 * block + core) * WIDTH, WIDTH), WIDTH)
        return (
            dot(og_all[block], w_ref[:, columns], 1, 1),
            dot(og_all[block], w_other[block], 1, 1),
        )

    loads["w"].wait()
    arrived(weights)
    mine, theirs = cotangent(0)
    steps = ((0, 2), (1, 6), (2, 1), (3, 7)) if relayed else enumerate(straight)
    for n, to in steps:
        if not relayed or n > 1:
            gathers[n].wait_recv()
        more, more_theirs = cotangent(-to)
        mine, theirs = mine + more, theirs + more_theirs
    if relayed:
        for came, block in (((5,), -3), ((7,), 3), ((4, 6), 4)):
            for n in came:
                gathers[n].wait_recv()
            more, more_theirs = cotangent(block)
            mine, theirs = mine + more, theirs + more_theirs
    grad_theirs[...] = theirs
    swap = remote(grad_theirs, grad_other, swap_send.at[0], swap_recv.at[0], partner)

    arrived(second)
    acc, acc_norm = zero_block, zero_row
    for i in range(Y):
        norm, still_open = small_of(f_buf2, i)
        counts = y_row > i
        acc = jnp.where(counts, unpack(f_buf2, i) + still_open * acc, acc)
        acc_norm = jnp.where(counts, norm + still_open * acc_norm, acc_norm)
    norm_in = zero_row
    for i in range(X):
        norm, start = small_of(f_buf1, i)
        opened = 1.0 - start
        acc, acc_norm = opened * acc, opened * acc_norm
        f_msg3[i] = acc.astype(BF16)
        norm_in = jnp.where(x_row == i, acc_norm, norm_in)
        acc, acc_norm = acc + unpack(f_buf1, i), acc_norm + norm
    f_in[here, :] = f_msg3[x]
    third = along_x(2, lambda to: f_msg3.at[to], f_in.at[here, :])

    scaled = sigq * norm_in
    inverse = both(
        lambda h: jnp.broadcast_to(
            1.0 / (jnp.sum(scaled[:, h], axis=1, keepdims=True) + 1.0), (LENGTH, DH)
        )
    )

    swap.wait_recv()
    grad = jnp.where(live, (mine + grad_other[...]).astype(BF16).astype(F32), 0.0)
    read_grad = gate * grad
    local_grad = ((1.0 - gate) * grad).astype(BF16)
    numer_grad = (read_grad * inverse).astype(BF16)
    state_grad = both(lambda h: dot(sigq_ref[:, h], numer_grad[:, h], 0, 0)).astype(BF16)
    for i in range(X):
        pack(b_msg1, i, state_grad[i * rows : (i + 1) * rows])
    b_buf1[x] = b_msg1[x]
    b_first = along_x(3, lambda to: b_msg1.at[to], b_buf1.at[x])

    arrived(third)
    read = both(lambda h: dot(sigq_ref[:, h], f_in[:, h], 1, 0)) * inverse
    mixed = jnp.where(live, gate * read + (1.0 - gate) * local_ref[...], 0.0)
    mixed_ref[...] = mixed.astype(BF16)
    mixing = remote(mixed_ref, mixed_other, swap_send.at[1], swap_recv.at[1], partner)

    product = read_grad * read
    denom_grad = -inverse * both(
        lambda h: jnp.broadcast_to(jnp.sum(product[:, h], axis=1, keepdims=True), (LENGTH, DH))
    )
    n_msg1[...] = small_rows(jnp.sum(sigq * denom_grad, axis=0, keepdims=True), flag)
    n_buf1[x] = n_msg1[...]
    n_first = along_x(6, lambda to: n_msg1, n_buf1.at[x])

    for j in range(Z):
        columns = pl.ds(pl.multiple_of((2 * z_at(j) + core) * WIDTH, WIDTH), WIDTH)
        part_ref[j] = dot(mixed_ref[...], w_ref[:, columns], 1, 0)

    arrived(b_first)
    acc = zero_block
    for i in range(X - 1, -1, -1):
        _, start = small_of(f_buf1, i)
        acc = (1.0 - start) * (acc + unpack(b_buf1, i))
    pack(b_msg2, 0, acc.astype(BF16))
    b_buf2[y] = b_msg2[0]
    b_second = along_y(4, b_msg2.at[0], b_buf2.at[y])

    mixing.wait_recv()
    reduces = {}

    def whole(j):
        j = j % Z
        return part_ref[j] + dot(mixed_other[...], w_other[z_at(j)], 1, 0)

    def reduce(n, value, part, to):
        rs_send[n, part] = value.astype(BF16)
        reduces[n] = remote(
            rs_send.at[n, part],
            rs_recv.at[n, part],
            rs_send_sem.at[n],
            rs_recv_sem.at[n],
            z_peer(to),
        )

    if relayed:
        across = whole(4)
        reduce(4, across[upper], upper, 2)
        reduce(6, across[lower], lower, -2)
        reduce(5, whole(3), full, 1)
        reduce(7, whole(-3), full, -1)
        reduce(2, whole(1), full, 1)
        reduce(3, whole(-1), full, -1)
        part_ref[2] = whole(2)
        part_ref[6] = whole(6)
    else:
        for n, to in enumerate(straight):
            reduce(n, whole(to), full, to)
    part_ref[0] = whole(0)

    parts = []
    for n in range(2):
        h = slice(n * DH, (n + 1) * DH)
        probs = probs_ref[n]
        probs_grad = dot(local_grad[:, h], v_ref[:, h], 1, 1)
        inner = jnp.sum(probs_grad * probs, axis=1, keepdims=True)
        scores_grad = (probs * (probs_grad - inner) * SCALE).astype(BF16)
        parts.append(
            (
                dot(scores_grad, k_ref[:, h], 1, 0)
                + (dot(numer_grad[:, h], f_in[:, h], 1, 1) + denom_grad[:, h] * norm_in[:, h])
                * phi_slope(q_ref[:, h].astype(F32)),
                dot(scores_grad, q_ref[:, h], 0, 0),
                dot(probs.astype(BF16), local_grad[:, h], 0, 0),
            )
        )
    stores = []

    def store(n, value, target):
        results[n] = value.astype(BF16)
        one = pltpu.make_async_copy(results.at[n], target, store_sem.at[n])
        one.start()
        stores.append(one)

    store(1, jnp.concatenate([parts[0][0], parts[1][0]], axis=1), dq_hbm)
    key_part = jnp.concatenate([parts[0][1], parts[1][1]], axis=1)
    value_part = jnp.concatenate([parts[0][2], parts[1][2]], axis=1)

    arrived(n_first)
    acc_norm = zero_row
    for i in range(X - 1, -1, -1):
        _, start = small_of(f_buf1, i)
        acc_norm = (1.0 - start) * (acc_norm + split_small(n_buf1[i])[0])
    n_msg2[...] = small_rows(acc_norm, flag)
    n_buf2[y] = n_msg2[...]
    n_second = along_y(7, n_msg2, n_buf2.at[y])

    arrived(b_second)
    acc = zero_block
    for i in range(Y - 1, -1, -1):
        _, still_open = small_of(f_buf2, i)
        acc = jnp.where(y_row < i, unpack(b_buf2, i) + still_open * acc, acc)
    for i in range(X - 1, -1, -1):
        _, start = small_of(f_buf1, i)
        b_msg3[i] = acc.astype(BF16)
        acc = (1.0 - start) * (acc + unpack(b_buf1, i))
    b_in[here, :] = b_msg3[x]
    b_third = along_x(5, lambda to: b_msg3.at[to], b_in.at[here, :])

    if relayed:
        for n, straight_on, across, part, to in ((0, 5, 4, upper, 2), (1, 7, 6, lower, -2)):
            reduces[straight_on].wait_recv()
            reduces[across].wait_recv()
            j = to % Z
            part_ref[j] = part_ref[j] + rs_recv[straight_on].astype(F32)
            part_ref[j, part] = part_ref[j, part] + rs_recv[across, part].astype(F32)
            reduce(n, part_ref[j], full, to)

    arrived(n_second)
    acc_norm = zero_row
    for i in range(Y - 1, -1, -1):
        _, still_open = small_of(f_buf2, i)
        acc_norm = jnp.where(
            y_row < i, split_small(n_buf2[i])[0] + still_open * acc_norm, acc_norm
        )
    norm_back = zero_row
    for i in range(X - 1, -1, -1):
        _, start = small_of(f_buf1, i)
        norm_back = jnp.where(x_row == i, acc_norm, norm_back)
        acc_norm = (1.0 - start) * (acc_norm + split_small(n_buf1[i])[0])

    arrived(b_third)
    k_float = k_ref[...].astype(F32)
    key_more = (both(lambda h: dot(v_ref[:, h], b_in[:, h], 1, 1)) + norm_back) * phi_slope(k_float)
    store(2, key_part + jnp.where(live, key_more, 0.0), dk_hbm)
    sigk_low = jnp.where(live, phi(k_float), 0.0).astype(BF16)
    store(3, value_part + both(lambda h: dot(sigk_low[:, h], b_in[:, h], 1, 0)), dv_hbm)

    total = part_ref[0]
    for n in (2, 3, 0, 1) if relayed else range(Z - 1):
        reduces[n].wait_recv()
        total = total + rs_recv[n].astype(F32)
    store(0, total, out_hbm)

    for one in sent:
        one.wait_send()
    for one in stores:
        one.wait()


def store_all(*refs):
    sources, targets, held, sem = refs[:4], refs[4:8], refs[8], refs[9]
    loads = [pltpu.make_async_copy(sources[n], held.at[n], sem.at[0, n]) for n in range(4)]
    stores = [pltpu.make_async_copy(held.at[n], targets[n], sem.at[1, n]) for n in range(4)]
    for one in loads:
        one.start()
    for load, one in zip(loads, stores):
        load.wait()
        one.start()
    for one in stores:
        one.wait()


def build(mesh, X):
    Y, Z = mesh.shape["seq"] // X, mesh.shape["head"] // 2
    rows = LENGTH // X
    dma = pltpu.SemaphoreType.DMA

    def block(*lead):
        return pltpu.VMEM((*lead, LENGTH, WIDTH), BF16)

    def wide(*lead):
        return pltpu.VMEM((*lead, LENGTH, WIDTH), F32)

    def message(n, count):
        return pltpu.VMEM((n, count, DH), BF16)

    most = max(X, Y)
    full = 2 * rows + SMALL
    scratch = [
        pltpu.SMEM((2,), F32),
        pltpu.SMEM((1,), jnp.int32),
        pltpu.SMEM((1,), jnp.int32),
        block(),
        block(),
        block(),
        block(Z),
        pltpu.VMEM((WIDTH, 2 * Z * WIDTH), BF16),
        pltpu.VMEM((Z, WIDTH, WIDTH), BF16),
        block(4),
        pltpu.VMEM((2, LENGTH, LENGTH), F32),
        wide(),
        block(),
        wide(),
        block(),
        block(),
        wide(),
        wide(),
        wide(Z),
        block(8),
        block(8),
        message(X, full),
        message(X, full),
        message(1, full),
        message(Y, full),
        pltpu.VMEM((X, rows, WIDTH), BF16),
        block(),
        message(X, 2 * rows),
        message(X, 2 * rows),
        message(1, 2 * rows),
        message(Y, 2 * rows),
        pltpu.VMEM((X, rows, WIDTH), BF16),
        block(),
        pltpu.VMEM((SMALL, DH), BF16),
        message(X, SMALL),
        pltpu.VMEM((SMALL, DH), BF16),
        message(Y, SMALL),
        dma((8,)),
        dma((4,)),
        dma((8, most)),
        dma((8, most)),
        dma((8,)),
        dma((8,)),
        dma((Z,)),
        dma((Z,)),
        dma((2,)),
        dma((2,)),
        dma((8,)),
        dma((8,)),
    ]

    def shards(queries, keys, values, gate, out_weight, out_grad, valid, starts):
        one = jax.ShapeDtypeStruct((LENGTH, WIDTH), BF16)
        results = pl.pallas_call(
            functools.partial(layer, (X, Y, Z)),
            out_shape=(one,) * 4,
            in_specs=[pl.BlockSpec(memory_space=pltpu.HBM)] * 8,
            out_specs=(pl.BlockSpec(memory_space=pl.ANY),) * 4,
            scratch_shapes=scratch,
            compiler_params=pltpu.CompilerParams(
                collective_id=0, has_side_effects=True, vmem_limit_bytes=63 * 1024 * 1024
            ),
            name="layer",
        )(gate, valid, starts, queries, keys, values, out_grad, out_weight)
        return pl.pallas_call(
            store_all,
            out_shape=(one,) * 4,
            in_specs=[pl.BlockSpec(memory_space=pl.ANY)] * 4,
            out_specs=(pl.BlockSpec(memory_space=pltpu.HBM),) * 4,
            scratch_shapes=[pltpu.VMEM((4, LENGTH, WIDTH), BF16), dma((2, 4))],
            compiler_params=pltpu.CompilerParams(vmem_limit_bytes=63 * 1024 * 1024),
            name="store_all",
        )(*results)

    placed = (
        P("seq", "head"),
        P("seq", "head"),
        P("seq", "head"),
        P("head"),
        P("head", None),
        P("seq", "head"),
        P("seq"),
        P("seq"),
    )
    return jax.shard_map(
        shards, mesh=mesh, in_specs=placed, out_specs=(P("seq", "head"),) * 4, check_vma=False
    )


def solution(mesh):
    return build(mesh, 8)
```

time: 62.7 us -> 57 us (0.909)
  Pallas kernels: 60.6 us -> 54.9 us
    pallas_call x1, Pallas kernels: 58.9 us -> 53.2 us  [shards(): pl.pallas_call(functools.partial(layer, (X, Y, Z)), out_shape=(one,) * 4,...]
where the time goes in v3:
time: 57 us; the launch traced here: 56.8 us
  Pallas kernels  54.9 us (96%)
  between operations  1.93 us (3%)
    pallas_call x1, Pallas kernels, shards(): pl.pallas_call(functools.partial(layer, (X, Y, Z)), out_shape=(one,) * 4,...  53.2 us
    pallas_call x1, Pallas kernels, shards(): pl.pallas_call(store_all, out_shape=(one,) * 4, in_specs=[pl.BlockSpec(me...  1.63 us

profile of v3, /device:TPU:1, one launch (start us, length us, event | category | flops | bytes accessed | tf_op | source)
XLA Modules:
  0.0 56.8 jit_solution(10880484908754222638)
XLA Ops:
  1.9 53.2 %layer.1 = (bf16[128,256]{1,0:T(8,128)(2,1)}, bf16[128,256]{1,0:T(8,128)(2,1)}, bf16[128,256]{1,0:T(8,128)(2,1)}, bf16[128,256]{1,0:T(8,128)(2,1)}) custom-call(f32[2]{0:T(128)} %gate_hbm.1, s32[1]{0:T(128)S(6)} %copy.12.valid_hbm, s32[1]{0:T(128)S(6)} %copy.13.starts_hbm, bf16[128,256]{1,0:T(8,128)(2,1)} %q_hbm.1, bf16[128,256]{1,0:T(8,128)(2,1)} %k_hbm.1, ...), custom_call_target="tpu_custom_call" | custom-call | tf_op jit(solution)/shard_map/layer/pallas_call | solution.py:587
  55.2 1.6 %store_all.1 = (bf16[128,256]{1,0:T(8,128)(2,1)}, bf16[128,256]{1,0:T(8,128)(2,1)}, bf16[128,256]{1,0:T(8,128)(2,1)}, bf16[128,256]{1,0:T(8,128)(2,1)}) custom-call(bf16[128,256]{1,0:T(8,128)(2,1)} %get-tuple-element.8.refs_0_, bf16[128,256]{1,0:T(8,128)(2,1)} %get-tuple-element.9.refs_1_, bf16[128,256]{1,0:T(8,128)(2,1)} %get-tuple-element.10.refs_2_, ...), custom_call_target="tpu_custom_call" | custom-call | tf_op jit(solution)/shard_map/store_all/pallas_call | solution.py:598

commit v4 on v3

v4 whole, which is shorter than its diff:
```python
import functools

import jax
import jax.numpy as jnp
from jax import lax
from jax.experimental import pallas as pl
from jax.experimental.pallas import tpu as pltpu
from jax.sharding import PartitionSpec as P

DH = 128
LENGTH = 128
WIDTH = 2 * DH
SMALL = 16
SCALE = DH ** (-0.5)
MESH = pl.DeviceIdType.MESH
F32, BF16 = jnp.float32, jnp.bfloat16


def dot(a, b, contract_a, contract_b):
    return lax.dot_general(
        a, b, (((contract_a,), (contract_b,)), ((), ())), preferred_element_type=F32
    )


def phi(x):
    return jnp.where(x > 0, x + 1.0, jnp.exp(jnp.minimum(x, 0.0)))


def phi_slope(x):
    return jnp.where(x > 0, 1.0, jnp.where(x == 0, 0.5, jnp.exp(jnp.minimum(x, 0.0))))


def both(one):
    return jnp.concatenate([one(slice(0, DH)), one(slice(DH, WIDTH))], axis=1)


def small_rows(norm, flag):
    high = norm.astype(BF16).astype(F32)
    low = norm - high
    at = lax.broadcasted_iota(jnp.int32, (SMALL, DH), 0)
    rows = jnp.zeros((SMALL, DH), F32)
    for n, row in enumerate(
        (high[:, :DH], high[:, DH:], low[:, :DH], low[:, DH:], flag[:, :DH])
    ):
        rows = jnp.where(at == n, row, rows)
    return rows.astype(BF16)


def split_small(small):
    small = small.astype(F32)
    norm = jnp.concatenate([small[0:1] + small[2:3], small[1:2] + small[3:4]], axis=1)
    return norm, jnp.concatenate([small[4:5], small[4:5]], axis=1)


def layer(
    sizes,
    valid_ref,
    starts_ref,
    gate_hbm,
    q_hbm,
    k_hbm,
    v_hbm,
    og_hbm,
    w_hbm,
    out_ref,
    dq_ref,
    dk_ref,
    dv_ref,
    gate_ref,
    q_ref,
    k_ref,
    v_ref,
    og_all,
    w_blocks,
    probs_ref,
    local_ref,
    sigq_ref,
    read_ref,
    mixed_ref,
    mixed_other,
    grad_theirs,
    grad_other,
    part_ref,
    rs_send,
    rs_recv,
    f_msg1,
    f_buf1,
    f_msg2,
    f_buf2,
    f_msg3,
    f_in,
    b_msg1,
    b_buf1,
    b_msg2,
    b_buf2,
    b_msg3,
    b_in,
    s_msg1,
    s_buf1,
    s_msg2,
    s_buf2,
    n_msg1,
    n_buf1,
    n_msg2,
    n_buf2,
    load_sem,
    own_sem,
    scan_send,
    scan_recv,
    ag_send,
    ag_recv,
    w_send,
    w_recv,
    swap_send,
    swap_recv,
    rs_send_sem,
    rs_recv_sem,
):
    X, Y, Z = sizes
    rows = LENGTH // X
    half = LENGTH // 2
    seq, head = lax.axis_index("seq"), lax.axis_index("head")
    y, x = lax.div(seq, X), lax.rem(seq, X)
    z, core = lax.div(head, 2), lax.rem(head, 2)

    def x_peer(j):
        return (y * X + lax.rem(x + j, X), head)

    def y_peer(j):
        return (lax.rem(y + j, Y) * X + x, head)

    def z_at(j):
        return lax.rem(z + j + Z, Z)

    def z_peer(j):
        return (seq, z_at(j) * 2 + core)

    partner = (seq, z * 2 + (1 - core))
    sent = []

    def remote(src, dst, send, recv, peer):
        one = pltpu.make_async_remote_copy(
            src_ref=src,
            dst_ref=dst,
            send_sem=send,
            recv_sem=recv,
            device_id=peer,
            device_id_type=MESH,
        )
        one.start()
        sent.append(one)
        return one

    loads = {}
    for n, (name, src, dst) in enumerate(
        (
            ("og", og_hbm, og_all.at[z]),
            ("k", k_hbm, k_ref),
            ("v", v_hbm, v_ref),
            ("gate", gate_hbm, gate_ref),
            ("q", q_hbm, q_ref),
        )
    ):
        loads[name] = pltpu.make_async_copy(src, dst, load_sem.at[n])
        loads[name].start()

    barrier = pltpu.get_barrier_semaphore()
    peers = [x_peer(j) for j in range(1, X)] + [y_peer(j) for j in range(1, Y)]
    relayed = Z == 8
    straight = (2, 6, 1, 7) if relayed else tuple(range(1, Z))
    peers += [z_peer(j) for j in straight] + [partner]
    for peer in peers:
        pl.semaphore_signal(barrier, inc=1, device_id=peer, device_id_type=MESH)

    def far_first(n):
        return sorted(range(1, n), key=lambda j: -min(j, n - j))

    def along_x(phase, source, target):
        return [
            remote(
                source(lax.rem(x + j, X)),
                target,
                scan_send.at[phase, j],
                scan_recv.at[phase, j],
                x_peer(j),
            )
            for j in far_first(X)
        ]

    def along_y(phase, source, target):
        return [
            remote(source, target, scan_send.at[phase, j], scan_recv.at[phase, j], y_peer(j))
            for j in far_first(Y)
        ]

    def arrived(copies):
        for one in copies:
            one.wait_recv()

    def pack(ref, place, block):
        ref[place, 0:rows, :] = block[:, :DH]
        ref[place, rows : 2 * rows, :] = block[:, DH:]

    def unpack(ref, place):
        return jnp.concatenate(
            [ref[place, 0:rows, :], ref[place, rows : 2 * rows, :]], axis=1
        ).astype(F32)

    zero_block, zero_row = jnp.zeros((rows, WIDTH), F32), jnp.zeros((1, WIDTH), F32)
    x_row, y_row = jnp.full((1, WIDTH), x, jnp.int32), jnp.full((1, WIDTH), y, jnp.int32)
    here = pl.ds(pl.multiple_of(x * rows, rows), rows)

    upper, lower, full = slice(0, half), slice(half, LENGTH), slice(0, LENGTH)

    def gather(n, block, part, to):
        piece = og_all.at[z_at(block), part]
        return remote(piece, piece, ag_send.at[n], ag_recv.at[n], z_peer(to))

    pl.semaphore_wait(barrier, len(peers))
    loads["og"].wait()
    gathers = {n: gather(n, 0, full, to) for n, to in enumerate(straight)}

    live = lax.broadcasted_iota(jnp.int32, (LENGTH, WIDTH), 0) < valid_ref[0]
    flag = jnp.full((1, WIDTH), starts_ref[0], jnp.int32).astype(F32)
    loads["k"].wait()
    sigk = jnp.where(live, phi(k_ref[...].astype(F32)), 0.0)
    s_msg1[...] = small_rows(jnp.sum(sigk, axis=0, keepdims=True), flag)
    s_buf1[x] = s_msg1[...]
    s_first = along_x(8, lambda to: s_msg1, s_buf1.at[x])
    sigk_low = sigk.astype(BF16)
    loads["v"].wait()
    state = both(lambda h: dot(sigk_low[:, h], v_ref[:, h], 0, 0)).astype(BF16)
    for i in range(X):
        pack(f_msg1, i, state[i * rows : (i + 1) * rows])
    f_buf1[x] = f_msg1[x]
    first = along_x(0, lambda to: f_msg1.at[to], f_buf1.at[x])

    weights, own_weights = [], []
    for i in range(Z):
        columns = pl.ds(pl.multiple_of((2 * i + 1 - core) * WIDTH, WIDTH), WIDTH)
        weights.append(
            remote(
                w_hbm.at[:, columns],
                w_blocks.at[i, WIDTH:, :],
                w_send.at[i],
                w_recv.at[i],
                partner,
            )
        )
    for i in range(Z):
        columns = pl.ds(pl.multiple_of((2 * i + core) * WIDTH, WIDTH), WIDTH)
        own_weights.append(
            pltpu.make_async_copy(w_hbm.at[:, columns], w_blocks.at[i, 0:WIDTH, :], own_sem.at[i])
        )
        own_weights[i].start()

    loads["gate"].wait()
    lanes = lax.broadcasted_iota(jnp.int32, (1, WIDTH), 1)
    logit = jnp.where(
        lanes < DH, jnp.full((1, WIDTH), gate_ref[0], F32), jnp.full((1, WIDTH), gate_ref[1], F32)
    )
    gate = 1.0 / (1.0 + jnp.exp(-logit))

    loads["q"].wait()
    row = lax.broadcasted_iota(jnp.int32, (LENGTH, LENGTH), 0)
    col = lax.broadcasted_iota(jnp.int32, (LENGTH, LENGTH), 1)
    allowed = (col <= row) & (col < valid_ref[0])

    def attend(n):
        h = slice(n * DH, (n + 1) * DH)
        scores = dot(q_ref[:, h], k_ref[:, h], 1, 1) * SCALE
        scores = jnp.where(allowed, scores, -1e30)
        expo = jnp.exp(scores - jnp.max(scores, axis=1, keepdims=True))
        probs = expo / jnp.sum(expo, axis=1, keepdims=True)
        probs_ref[n] = probs
        local_ref[:, h] = dot(probs.astype(BF16), v_ref[:, h], 1, 0)

    attend(0)
    if relayed:
        for n, (came, block, part, to) in enumerate(
            ((0, -2, upper, 2), (0, -2, full, 1), (1, 2, lower, -2), (1, 2, full, -1))
        ):
            if n % 2 == 0:
                gathers[came].wait_recv()
            gathers[4 + n] = gather(4 + n, block, part, to)

    arrived(s_first)
    row_small = [split_small(s_buf1[i]) for i in range(X)]
    opened = [1.0 - start for _, start in row_small]
    acc_norm, still_open = zero_row, jnp.ones((1, WIDTH), F32)
    for i in range(X):
        acc_norm = opened[i] * acc_norm + row_small[i][0]
        still_open = still_open * opened[i]
    s_msg2[...] = small_rows(acc_norm, still_open)
    s_buf2[y] = s_msg2[...]
    s_second = along_y(9, s_msg2, s_buf2.at[y])

    attend(1)

    arrived(first)
    acc = zero_block
    for i in range(X):
        acc = opened[i] * acc + unpack(f_buf1, i)
    pack(f_msg2, 0, acc.astype(BF16))
    f_buf2[y] = f_msg2[0]
    second = along_y(1, f_msg2.at[0], f_buf2.at[y])

    sigq = phi(q_ref[...].astype(F32))
    sigq_ref[...] = sigq.astype(BF16)

    def cotangent(j):
        block = z_at(j)
        return dot(w_blocks[block], og_all[block], 1, 1)

    for one in own_weights:
        one.wait()
    arrived(weights)
    grads = cotangent(0)
    steps = ((0, 2), (1, 6), (2, 1), (3, 7)) if relayed else enumerate(straight)
    for n, to in steps:
        if not relayed or n > 1:
            gathers[n].wait_recv()
        grads = grads + cotangent(-to)
    if relayed:
        for came, block in (((5,), -3), ((7,), 3), ((4, 6), 4)):
            for n in came:
                gathers[n].wait_recv()
            grads = grads + cotangent(block)
    mine = grads[:WIDTH]
    grad_theirs[...] = grads[WIDTH:]
    swap = remote(grad_theirs, grad_other, swap_send.at[0], swap_recv.at[0], partner)

    arrived(s_second)
    rows_small = [split_small(s_buf2[i]) for i in range(Y)]
    acc_norm, norm_in = zero_row, zero_row
    for i in range(Y):
        norm, still_open = rows_small[i]
        acc_norm = jnp.where(y_row > i, norm + still_open * acc_norm, acc_norm)
    for i in range(X):
        acc_norm = opened[i] * acc_norm
        norm_in = jnp.where(x_row == i, acc_norm, norm_in)
        acc_norm = acc_norm + row_small[i][0]
    scaled = sigq * norm_in
    inverse = both(
        lambda h: jnp.broadcast_to(
            1.0 / (jnp.sum(scaled[:, h], axis=1, keepdims=True) + 1.0), (LENGTH, DH)
        )
    )

    arrived(second)
    acc = zero_block
    for i in range(Y):
        acc = jnp.where(y_row > i, unpack(f_buf2, i) + rows_small[i][1] * acc, acc)
    for i in range(X):
        acc = opened[i] * acc
        f_msg3[i] = acc.astype(BF16)
        acc = acc + unpack(f_buf1, i)
    f_in[here, :] = f_msg3[x]
    third = along_x(2, lambda to: f_msg3.at[to], f_in.at[here, :])

    gated = jnp.where(live, gate * inverse, 0.0)
    mixed_local = jnp.where(live, (1.0 - gate) * local_ref[...], 0.0)

    swap.wait_recv()
    grad = jnp.where(live, (mine + grad_other[...]).T.astype(BF16).astype(F32), 0.0)
    read_grad = gate * grad
    local_grad = ((1.0 - gate) * grad).astype(BF16)
    numer_grad = (gated * grad).astype(BF16)
    state_grad = both(lambda h: dot(sigq_ref[:, h], numer_grad[:, h], 0, 0)).astype(BF16)
    for i in range(X):
        pack(b_msg1, i, state_grad[i * rows : (i + 1) * rows])
    b_buf1[x] = b_msg1[x]
    b_first = along_x(3, lambda to: b_msg1.at[to], b_buf1.at[x])

    arrived(third)
    numer = both(lambda h: dot(sigq_ref[:, h], f_in[:, h], 1, 0))
    mixed_ref[...] = (gated * numer + mixed_local).astype(BF16)
    mixing = remote(mixed_ref, mixed_other, swap_send.at[1], swap_recv.at[1], partner)

    product = read_grad * (numer * inverse)
    denom_grad = -inverse * both(
        lambda h: jnp.broadcast_to(jnp.sum(product[:, h], axis=1, keepdims=True), (LENGTH, DH))
    )
    n_msg1[...] = small_rows(jnp.sum(sigq * denom_grad, axis=0, keepdims=True), flag)
    n_buf1[x] = n_msg1[...]
    n_first = along_x(6, lambda to: n_msg1, n_buf1.at[x])

    arrived(b_first)
    acc = zero_block
    for i in range(X - 1, -1, -1):
        acc = opened[i] * (acc + unpack(b_buf1, i))
    pack(b_msg2, 0, acc.astype(BF16))
    b_buf2[y] = b_msg2[0]
    b_second = along_y(4, b_msg2.at[0], b_buf2.at[y])

    reduce_order = [j for j in (4, 3, 5, 1, 7, 2, 6, 0) if relayed] or list(range(Z))
    for j in reduce_order[:3]:
        part_ref[j] = dot(mixed_ref[...], w_blocks[z_at(j), 0:WIDTH, :], 1, 0)

    mixing.wait_recv()
    reduces = {}

    def whole(j):
        j = j % Z
        block = z_at(j)
        if j in reduce_order[:3]:
            part = part_ref[j]
        else:
            part = dot(mixed_ref[...], w_blocks[block, 0:WIDTH, :], 1, 0)
        return part + dot(mixed_other[...], w_blocks[block, WIDTH:, :], 1, 0)

    def reduce(n, value, part, to):
        rs_send[n, part] = value.astype(BF16)
        reduces[n] = remote(
            rs_send.at[n, part],
            rs_recv.at[n, part],
            rs_send_sem.at[n],
            rs_recv_sem.at[n],
            z_peer(to),
        )

    if relayed:
        across = whole(4)
        reduce(4, across[upper], upper, 2)
        reduce(6, across[lower], lower, -2)
        reduce(5, whole(3), full, 1)
        reduce(7, whole(-3), full, -1)
        reduce(2, whole(1), full, 1)
        reduce(3, whole(-1), full, -1)
        part_ref[2] = whole(2)
        part_ref[6] = whole(6)
    else:
        for n, to in enumerate(straight):
            reduce(n, whole(to), full, to)
    part_ref[0] = whole(0)

    parts = []
    for n in range(2):
        h = slice(n * DH, (n + 1) * DH)
        probs = probs_ref[n]
        probs_grad = dot(local_grad[:, h], v_ref[:, h], 1, 1)
        inner = jnp.sum(probs_grad * probs, axis=1, keepdims=True)
        scores_grad = (probs * (probs_grad - inner) * SCALE).astype(BF16)
        parts.append(
            (
                dot(scores_grad, k_ref[:, h], 1, 0)
                + (dot(numer_grad[:, h], f_in[:, h], 1, 1) + denom_grad[:, h] * norm_in[:, h])
                * phi_slope(q_ref[:, h].astype(F32)),
                dot(scores_grad, q_ref[:, h], 0, 0),
                dot(probs.astype(BF16), local_grad[:, h], 0, 0),
            )
        )
    dq_ref[...] = jnp.concatenate([parts[0][0], parts[1][0]], axis=1).astype(BF16)
    key_part = jnp.concatenate([parts[0][1], parts[1][1]], axis=1)
    value_part = jnp.concatenate([parts[0][2], parts[1][2]], axis=1)

    arrived(n_first)
    acc_norm = zero_row
    for i in range(X - 1, -1, -1):
        acc_norm = opened[i] * (acc_norm + split_small(n_buf1[i])[0])
    n_msg2[...] = small_rows(acc_norm, flag)
    n_buf2[y] = n_msg2[...]
    n_second = along_y(7, n_msg2, n_buf2.at[y])

    arrived(b_second)
    acc = zero_block
    for i in range(Y - 1, -1, -1):
        acc = jnp.where(y_row < i, unpack(b_buf2, i) + rows_small[i][1] * acc, acc)
    for i in range(X - 1, -1, -1):
        b_msg3[i] = acc.astype(BF16)
        acc = opened[i] * (acc + unpack(b_buf1, i))
    b_in[here, :] = b_msg3[x]
    b_third = along_x(5, lambda to: b_msg3.at[to], b_in.at[here, :])

    if relayed:
        for n, straight_on, across, part, to in ((0, 5, 4, upper, 2), (1, 7, 6, lower, -2)):
            reduces[straight_on].wait_recv()
            reduces[across].wait_recv()
            j = to % Z
            part_ref[j] = part_ref[j] + rs_recv[straight_on].astype(F32)
            part_ref[j, part] = part_ref[j, part] + rs_recv[across, part].astype(F32)
            reduce(n, part_ref[j], full, to)

    arrived(n_second)
    acc_norm = zero_row
    for i in range(Y - 1, -1, -1):
        acc_norm = jnp.where(
            y_row < i, split_small(n_buf2[i])[0] + rows_small[i][1] * acc_norm, acc_norm
        )
    norm_back = zero_row
    for i in range(X - 1, -1, -1):
        norm_back = jnp.where(x_row == i, acc_norm, norm_back)
        acc_norm = opened[i] * (acc_norm + split_small(n_buf1[i])[0])

    k_float = k_ref[...].astype(F32)
    slope = jnp.where(live, phi_slope(k_float), 0.0)
    sigk_low = jnp.where(live, phi(k_float), 0.0).astype(BF16)
    key_part = key_part + norm_back * slope
    arrived(b_third)
    key_more = both(lambda h: dot(v_ref[:, h], b_in[:, h], 1, 1)) * slope
    dk_ref[...] = (key_part + key_more).astype(BF16)
    value_more = both(lambda h: dot(sigk_low[:, h], b_in[:, h], 1, 0))
    dv_ref[...] = (value_part + value_more).astype(BF16)

    total = part_ref[0]
    for n in (2, 3, 0, 1) if relayed else range(Z - 1):
        reduces[n].wait_recv()
        total = total + rs_recv[n].astype(F32)
    out_ref[...] = total.astype(BF16)

    for one in sent:
        one.wait_send()


def store_all(*refs):
    sources, targets, sem = refs[:4], refs[4:8], refs[8]
    stores = [pltpu.make_async_copy(sources[n], targets[n], sem.at[n]) for n in range(4)]
    for one in stores:
        one.start()
    for one in stores:
        one.wait()


def build(mesh, X):
    Y, Z = mesh.shape["seq"] // X, mesh.shape["head"] // 2
    rows = LENGTH // X
    dma = pltpu.SemaphoreType.DMA

    def block(*lead):
        return pltpu.VMEM((*lead, LENGTH, WIDTH), BF16)

    def wide(*lead):
        return pltpu.VMEM((*lead, LENGTH, WIDTH), F32)

    def message(n, count):
        return pltpu.VMEM((n, count, DH), BF16)

    def small_scratch():
        return [
            pltpu.VMEM((SMALL, DH), BF16),
            message(X, SMALL),
            pltpu.VMEM((SMALL, DH), BF16),
            message(Y, SMALL),
        ]

    most = max(X, Y)
    scratch = [
        pltpu.SMEM((2,), F32),
        block(),
        block(),
        block(),
        block(Z),
        pltpu.VMEM((Z, 2 * WIDTH, WIDTH), BF16),
        pltpu.VMEM((2, LENGTH, LENGTH), F32),
        wide(),
        block(),
        wide(),
        block(),
        block(),
        pltpu.VMEM((WIDTH, LENGTH), F32),
        pltpu.VMEM((WIDTH, LENGTH), F32),
        wide(Z),
        block(8),
        block(8),
        message(X, 2 * rows),
        message(X, 2 * rows),
        message(1, 2 * rows),
        message(Y, 2 * rows),
        pltpu.VMEM((X, rows, WIDTH), BF16),
        block(),
        message(X, 2 * rows),
        message(X, 2 * rows),
        message(1, 2 * rows),
        message(Y, 2 * rows),
        pltpu.VMEM((X, rows, WIDTH), BF16),
        block(),
        *small_scratch(),
        *small_scratch(),
        dma((5,)),
        dma((Z,)),
        dma((10, most)),
        dma((10, most)),
        dma((8,)),
        dma((8,)),
        dma((Z,)),
        dma((Z,)),
        dma((2,)),
        dma((2,)),
        dma((8,)),
        dma((8,)),
    ]

    def shards(queries, keys, values, gate, out_weight, out_grad, valid, starts):
        one = jax.ShapeDtypeStruct((LENGTH, WIDTH), BF16)
        results = pl.pallas_call(
            functools.partial(layer, (X, Y, Z)),
            out_shape=(one,) * 4,
            in_specs=[pl.BlockSpec(memory_space=pltpu.SMEM)] * 2
            + [pl.BlockSpec(memory_space=pltpu.HBM)] * 6,
            out_specs=(pl.BlockSpec(memory_space=pltpu.VMEM),) * 4,
            scratch_shapes=scratch,
            compiler_params=pltpu.CompilerParams(
                collective_id=0, has_side_effects=True, vmem_limit_bytes=32 * 1024 * 1024
            ),
            name="layer",
        )(
            valid,
            starts,
            *(
                pltpu.with_memory_space_constraint(a, pltpu.HBM)
                for a in (gate, queries, keys, values, out_grad, out_weight)
            ),
        )
        return pl.pallas_call(
            store_all,
            out_shape=(one,) * 4,
            in_specs=[pl.BlockSpec(memory_space=pltpu.VMEM)] * 4,
            out_specs=(pl.BlockSpec(memory_space=pltpu.HBM),) * 4,
            scratch_shapes=[dma((4,))],
            name="store_all",
        )(*(pltpu.with_memory_space_constraint(a, pltpu.VMEM) for a in results))

    placed = (
        P("seq", "head"),
        P("seq", "head"),
        P("seq", "head"),
        P("head"),
        P("head", None),
        P("seq", "head"),
        P("seq"),
        P("seq"),
    )
    return jax.shard_map(
        shards, mesh=mesh, in_specs=placed, out_specs=(P("seq", "head"),) * 4, check_vma=False
    )


def solution(mesh):
    return build(mesh, 8)
```

time: 57 us -> 54.8 us (0.961)
  Pallas kernels: 54.9 us -> 52.7 us
    pallas_call x1, Pallas kernels: 53.2 us -> 52 us  [shards(): pl.pallas_call(functools.partial(layer, (X, Y, Z)), out_shape=(one,) * 4,...]
    pallas_call x1, Pallas kernels: 1.63 us -> 0.73 us  [shards(): pl.pallas_call(store_all, out_shape=(one,) * 4, in_specs=[pl.BlockSpec(me...]
where the time goes in v4:
time: 54.8 us; the launch traced here: 54.6 us
  Pallas kernels  52.7 us (96%)
  between operations  1.93 us (4%)
    pallas_call x1, Pallas kernels, shards(): pl.pallas_call(functools.partial(layer, (X, Y, Z)), out_shape=(one,) * 4,...  52 us

profile of v4, /device:TPU:1, one launch (start us, length us, event | category | flops | bytes accessed | tf_op | source)
XLA Modules:
  0.0 54.6 jit_solution(9504039266181557734)
XLA Ops:
  1.9 52.0 %layer.1 = (bf16[128,256]{1,0:T(8,128)(2,1)S(1)}, bf16[128,256]{1,0:T(8,128)(2,1)S(1)}, bf16[128,256]{1,0:T(8,128)(2,1)S(1)}, bf16[128,256]{1,0:T(8,128)(2,1)S(1)}) custom-call(s32[1]{0:T(128)S(6)} %copy.12.valid_ref, s32[1]{0:T(128)S(6)} %copy.13.starts_ref, f32[2]{0:T(128)} %gate_hbm.1, bf16[128,256]{1,0:T(8,128)(2,1)} %q_hbm.1, bf16[128,256]{1,0:T(8,128)(2,1)} %k_hbm.1, ...), custom_call_target="tpu_custom_call" | custom-call | tf_op jit(solution)/shard_map/layer/pallas_call | solution.py:595
  53.9 0.7 %store_all.1 = (bf16[128,256]{1,0:T(8,128)(2,1)}, bf16[128,256]{1,0:T(8,128)(2,1)}, bf16[128,256]{1,0:T(8,128)(2,1)}, bf16[128,256]{1,0:T(8,128)(2,1)}) custom-call(bf16[128,256]{1,0:T(8,128)(2,1)S(1)} %get-tuple-element.8.refs_0_, bf16[128,256]{1,0:T(8,128)(2,1)S(1)} %get-tuple-element.9.refs_1_, bf16[128,256]{1,0:T(8,128)(2,1)S(1)} %get-tuple-element.10.refs_2_, ...), custom_call_target="tpu_custom_call" | custom-call | tf_op jit(solution)/shard_map/store_all/pallas_call | solution.py:614

commit v5 on v4

--- a/solution.py
+++ b/solution.py
@@ -385,6 +385,8 @@
     n_buf1[x] = n_msg1[...]
     n_first = along_x(6, lambda to: n_msg1, n_buf1.at[x])
 
+    early = len(sent)
+
     arrived(b_first)
     acc = zero_block
     for i in range(X - 1, -1, -1):
@@ -462,6 +464,15 @@
     n_buf2[y] = n_msg2[...]
     n_second = along_y(7, n_msg2, n_buf2.at[y])
 
+    if relayed:
+        for n, straight_on, across, part, to in ((0, 5, 4, upper, 2), (1, 7, 6, lower, -2)):
+            reduces[straight_on].wait_recv()
+            reduces[across].wait_recv()
+            j = to % Z
+            part_ref[j] = part_ref[j] + rs_recv[straight_on].astype(F32)
+            part_ref[j, part] = part_ref[j, part] + rs_recv[across, part].astype(F32)
+            reduce(n, part_ref[j], full, to)
+
     arrived(b_second)
     acc = zero_block
     for i in range(Y - 1, -1, -1):
@@ -472,15 +483,6 @@
     b_in[here, :] = b_msg3[x]
     b_third = along_x(5, lambda to: b_msg3.at[to], b_in.at[here, :])
 
-    if relayed:
-        for n, straight_on, across, part, to in ((0, 5, 4, upper, 2), (1, 7, 6, lower, -2)):
-            reduces[straight_on].wait_recv()
-            reduces[across].wait_recv()
-            j = to % Z
-            part_ref[j] = part_ref[j] + rs_recv[straight_on].astype(F32)
-            part_ref[j, part] = part_ref[j, part] + rs_recv[across, part].astype(F32)
-            reduce(n, part_ref[j], full, to)
-
     arrived(n_second)
     acc_norm = zero_row
     for i in range(Y - 1, -1, -1):
@@ -496,6 +498,8 @@
     slope = jnp.where(live, phi_slope(k_float), 0.0)
     sigk_low = jnp.where(live, phi(k_float), 0.0).astype(BF16)
     key_part = key_part + norm_back * slope
+    for one in sent[:early]:
+        one.wait_send()
     arrived(b_third)
     key_more = both(lambda h: dot(v_ref[:, h], b_in[:, h], 1, 1)) * slope
     dk_ref[...] = (key_part + key_more).astype(BF16)
@@ -508,7 +512,7 @@
         total = total + rs_recv[n].astype(F32)
     out_ref[...] = total.astype(BF16)
 
-    for one in sent:
+    for one in sent[early:]:
         one.wait_send()
 
 

time: 54.8 us -> 54.7 us (level)
  no operation moved by 1% of the time
where the time goes in v5:
time: 54.7 us; the launch traced here: 54.5 us
  Pallas kernels  52.6 us (96%)
  between operations  1.93 us (4%)
    pallas_call x1, Pallas kernels, shards(): pl.pallas_call(functools.partial(layer, (X, Y, Z)), out_shape=(one,) * 4,...  51.9 us

profile of v5, /device:TPU:1, one launch (start us, length us, event | category | flops | bytes accessed | tf_op | source)
XLA Modules:
  0.0 54.5 jit_solution(8466791399434390300)
XLA Ops:
  1.9 51.9 %layer.1 = (bf16[128,256]{1,0:T(8,128)(2,1)S(1)}, bf16[128,256]{1,0:T(8,128)(2,1)S(1)}, bf16[128,256]{1,0:T(8,128)(2,1)S(1)}, bf16[128,256]{1,0:T(8,128)(2,1)S(1)}) custom-call(s32[1]{0:T(128)S(6)} %copy.12.valid_ref, s32[1]{0:T(128)S(6)} %copy.13.starts_ref, f32[2]{0:T(128)} %gate_hbm.1, bf16[128,256]{1,0:T(8,128)(2,1)} %q_hbm.1, bf16[128,256]{1,0:T(8,128)(2,1)} %k_hbm.1, ...), custom_call_target="tpu_custom_call" | custom-call | tf_op jit(solution)/shard_map/layer/pallas_call | solution.py:599
  53.8 0.7 %store_all.1 = (bf16[128,256]{1,0:T(8,128)(2,1)}, bf16[128,256]{1,0:T(8,128)(2,1)}, bf16[128,256]{1,0:T(8,128)(2,1)}, bf16[128,256]{1,0:T(8,128)(2,1)}) custom-call(bf16[128,256]{1,0:T(8,128)(2,1)S(1)} %get-tuple-element.8.refs_0_, bf16[128,256]{1,0:T(8,128)(2,1)S(1)} %get-tuple-element.9.refs_1_, bf16[128,256]{1,0:T(8,128)(2,1)S(1)} %get-tuple-element.10.refs_2_, ...), custom_call_target="tpu_custom_call" | custom-call | tf_op jit(solution)/shard_map/store_all/pallas_call | solution.py:618
